TPU v7x, 32 devices: a whole 2x2x4 slice. The times are simulated.
32 devices in a mesh: rep: 16 (over z, x, core), shard: 2 (over y).
Axes of the slice: x: 2, y: 2, z: 4, core: 2. Of those that a mesh axis runs over, the one named last changes fastest.
Arguments:
- layer_input: bfloat16 [24576, 1024], P(('rep', 'shard')), may hold values from -6 to 6
- output_gradient: bfloat16 [24576, 1024], P(('rep', 'shard')), may hold values from -6 to 6
- routes: int32 [24576, 8], P(('rep', 'shard')), may hold values from 0 to 31, all different within a row; in each aligned block of 768 rows (0 to 767, 768 to 1535, ...) at most 240 rows name the same one
- sequence_adapter: int32 [16, 2], P('rep'), may hold values from 0 to 3
- attention_gain: float32 [1024], replicated, may hold values from 0.1 to 1.9
- experts_gain: float32 [1024], replicated, may hold values from 0.1 to 1.9
- project_weight: bfloat16 [1024, 2048], P(None, 'shard'), may hold values from -0.25 to 0.25
- output_weight: bfloat16 [1024, 1024], P('shard'), may hold values from -0.75 to 0.75
- router_weight: bfloat16 [1024, 32], P('shard'), may hold values from -0.09375 to 0.09375
- adapter_project_first: bfloat16 [1024, 192], P('shard'), may hold values from -0.1875 to 0.1875
- adapter_project_second: bfloat16 [64, 2048], P(None, 'shard'), may hold values from -0.75 to 0.75
- adapter_output_first: bfloat16 [1024, 64], P('shard'), may hold values from -0.75 to 0.75
- adapter_output_second: bfloat16 [64, 1024], P(None, 'shard'), may hold values from -0.75 to 0.75
- adapter_router_first: bfloat16 [1024, 64], P('shard'), may hold values from -0.1875 to 0.1875
- adapter_router_second: bfloat16 [64, 32], P(None, 'shard'), may hold values from -0.1875 to 0.1875
- expert_gate_up_weight: bfloat16 [32, 1024, 1024], P('shard'), may hold values from -0.1875 to 0.1875
- expert_down_weight: bfloat16 [32, 512, 1024], P('shard'), may hold values from -1 to 1
- adapter_expert_first: bfloat16 [32, 1024, 128], P('shard'), may hold values from -0.1875 to 0.1875
- adapter_expert_second: bfloat16 [32, 64, 1024], P('shard'), may hold values from -0.75 to 0.75
- adapter_expert_down_first: bfloat16 [32, 512, 64], P('shard'), may hold values from -0.25 to 0.25
- adapter_expert_down_second: bfloat16 [32, 64, 1024], P('shard'), may hold values from -1.5 to 1.5
Outputs:
- block_out: bfloat16 [24576, 1024], P(('rep', 'shard'))
- input_grad: bfloat16 [24576, 1024], P(('rep', 'shard'))
- grad_lora_in_qkv: float32 [1024, 192], P('shard')
- grad_lora_out_qkv: float32 [64, 2048], P(None, 'shard')
- grad_lora_in_out: float32 [1024, 64], P('shard')
- grad_lora_out_out: float32 [64, 1024], P(None, 'shard')
- grad_lora_in_router: float32 [1024, 64], P('shard')
- grad_lora_out_router: float32 [64, 32], P(None, 'shard')
- grad_lora_expert_in: float32 [32, 1024, 128], P('shard')
- grad_lora_expert_mid: float32 [32, 64, 1024], P('shard')
- grad_lora_expert_down_in: float32 [32, 512, 64], P('shard')
- grad_lora_expert_down_out: float32 [32, 64, 1024], P('shard')
Inputs may be any that keep to these rules, and one draw needn't show every extreme that they name: `routes`: each row names 8 different experts. Among the rows of one device no expert is named by more than 240 rows, and in some device's rows one expert is named by exactly 240.
All inputs are finite; a program needn't handle non-finite values.
Results may differ from a plain program's by a relative error of at most 0.024.
The roundings to bfloat16 on the way count: a program that leaves them out, or rounds other values in their place, can miss the bound.
Values may be sent and summed in bfloat16 or wider, within the bound.
A program may use at most 448 MiB of HBM per device.

v0:
```python
import math

import jax
import jax.numpy as jnp
from jax import lax
from jax.sharding import PartitionSpec as P

MODEL_WIDTH = 1024
QUERY_HEADS = 16
KEY_HEADS = 8
HEAD_SIZE = 64
EXPERT_COUNT = 32
EXPERT_HIDDEN = 512
TOPK = 8
ADAPTER_RANK = 16
ADAPTER_POOL = 4
PROMPT = 1024
CONT_LEN = 512


EPSILON = 1e-06
THETA = 10000.0
NEGATIVE = -1e30


def matmul(left_side, right_side):
    return jnp.dot(left_side, right_side, preferred_element_type=jnp.float32)


def matmul_back(left_side, right_side):
    return lax.dot_general(
        left_side, right_side, (((1,), (1,)), ((), ())), preferred_element_type=jnp.float32
    )


def matmul_rows(left_side, right_side):
    return lax.dot_general(
        left_side, right_side, (((0,), (0,)), ((), ())), preferred_element_type=jnp.float32
    )


def batched_apply(left_side, right_side):
    return lax.dot_general(
        left_side, right_side, (((2,), (1,)), ((0,), (0,))), preferred_element_type=jnp.float32
    )


def batched_backward(left_side, right_side):
    return lax.dot_general(
        left_side, right_side, (((2,), (2,)), ((0,), (0,))), preferred_element_type=jnp.float32
    )


def batched_row_set(left_side, right_side):
    return lax.dot_general(
        left_side, right_side, (((1,), (1,)), ((0,), (0,))), preferred_element_type=jnp.float32
    )


def adapter_rank_mask(onehot, copies):
    widened = jnp.repeat(onehot, ADAPTER_RANK, axis=-1)
    return jnp.concatenate([widened] * copies, axis=-1)


def token_layout(row_position):
    past_prompt = jnp.maximum(row_position - PROMPT, 0)
    sequence = jnp.where(row_position < PROMPT, 0, 1 + past_prompt // CONT_LEN)
    position = jnp.where(row_position < PROMPT, row_position, PROMPT + past_prompt % CONT_LEN)
    return (sequence, position)


def rotary_table(position):
    half_width = HEAD_SIZE // 2
    frequency = jnp.exp(
        jnp.arange(half_width, dtype=jnp.float32) * (-2.0 * math.log(THETA) / HEAD_SIZE)
    )
    angle_table = position.astype(jnp.float32)[:, None] * frequency[None, :]
    return (jnp.cos(angle_table), jnp.sin(angle_table))


def rotate_halves(values, cosine_table, sine_table):
    half_width = HEAD_SIZE // 2
    first_half = values[..., :half_width]
    second_half = values[..., half_width:]
    cos_heads = cosine_table[:, None, :]
    sin_heads = sine_table[:, None, :]
    return jnp.concatenate(
        [
            first_half * cos_heads - second_half * sin_heads,
            second_half * cos_heads + first_half * sin_heads,
        ],
        axis=-1,
    )


def norm_back(grad_in, values, inverse, gain_row):
    scaled = grad_in * gain_row
    normed = values * inverse
    return inverse * (scaled - normed * jnp.mean(scaled * normed, axis=-1, keepdims=True))


def visible_mask(seq_rows, pos_rows, seq_keys, pos_keys):
    return ((seq_keys[None, :] == 0) | (seq_keys[None, :] == seq_rows[:, None])) & (
        pos_keys[None, :] <= pos_rows[:, None]
    )


def slot_layout(route_rows, capacity):
    token_count = route_rows.shape[0]
    flat_routes = route_rows.reshape(-1)
    route_hits = (
        flat_routes[:, None] == jnp.arange(EXPERT_COUNT, dtype=jnp.int32)[None, :]
    ).astype(jnp.int32)
    slot_index = jnp.sum((jnp.cumsum(route_hits, axis=0) - 1) * route_hits, axis=1)
    target = flat_routes * capacity + slot_index
    assignment = jnp.arange(token_count * TOPK, dtype=jnp.int32)
    slot_assign = (
        jnp.full((EXPERT_COUNT * capacity,), token_count * TOPK, jnp.int32)
        .at[target]
        .set(assignment)
    )
    return (target, slot_assign)


def forward_block(
    query_tile, seq_rows, pos_rows, keys_heads, values_heads, seq_keys, pos_keys, score_scale
):
    row_sizes = query_tile.shape[0]
    visible = visible_mask(seq_rows, pos_rows, seq_keys, pos_keys)
    head_query_rows = query_tile.reshape(
        row_sizes, KEY_HEADS, QUERY_HEADS // KEY_HEADS, HEAD_SIZE
    ).transpose(1, 0, 2, 3)

    def forward_one_head(parts_list):
        head_query, head_keys, head_values = parts_list
        scores = (
            jnp.einsum("bgd,nd->gbn", head_query, head_keys, preferred_element_type=jnp.float32)
            * score_scale
        )
        scores = jnp.where(visible[None], scores, NEGATIVE)
        row_max = jnp.max(scores, axis=-1, keepdims=True)
        weights = jnp.exp(scores - row_max)
        weight_total = jnp.sum(weights, axis=-1, keepdims=True)
        probs = (weights / weight_total).astype(jnp.bfloat16)
        head_out = jnp.einsum("gbn,nd->bgd", probs, head_values, preferred_element_type=jnp.float32)
        return (head_out, (row_max + jnp.log(weight_total))[..., 0])

    head_outs, log_total = lax.map(forward_one_head, (head_query_rows, keys_heads, values_heads))
    return (
        head_outs.transpose(1, 0, 2, 3)
        .reshape(row_sizes, QUERY_HEADS * HEAD_SIZE)
        .astype(jnp.bfloat16),
        log_total,
    )


def backward_block(
    query_tile,
    gradient_block,
    log_total,
    seq_rows,
    pos_rows,
    keys_heads,
    values_heads,
    seq_keys,
    pos_keys,
    score_scale,
):
    row_sizes = query_tile.shape[0]
    groups_each_device = QUERY_HEADS // KEY_HEADS
    visible = visible_mask(seq_rows, pos_rows, seq_keys, pos_keys)
    head_query_rows = query_tile.reshape(
        row_sizes, KEY_HEADS, groups_each_device, HEAD_SIZE
    ).transpose(1, 0, 2, 3)
    head_gradient = gradient_block.reshape(
        row_sizes, KEY_HEADS, groups_each_device, HEAD_SIZE
    ).transpose(1, 0, 2, 3)

    def backward_one_head(parts_list):
        head_query, head_grad, head_total, head_keys, head_values = parts_list
        scores = (
            jnp.einsum("bgd,nd->gbn", head_query, head_keys, preferred_element_type=jnp.float32)
            * score_scale
        )
        scores = jnp.where(visible[None], scores, NEGATIVE)
        probs = jnp.exp(scores - head_total[..., None])
        grad_probs = jnp.einsum(
            "bgd,nd->gbn", head_grad, head_values, preferred_element_type=jnp.float32
        )
        delta_row = jnp.sum(grad_probs * probs, axis=-1, keepdims=True)
        grad_scores = (probs * (grad_probs - delta_row)).astype(jnp.bfloat16)
        grad_query = (
            jnp.einsum("gbn,nd->bgd", grad_scores, head_keys, preferred_element_type=jnp.float32)
            * score_scale
        )
        grad_keys = (
            jnp.einsum("gbn,bgd->nd", grad_scores, head_query, preferred_element_type=jnp.float32)
            * score_scale
        )
        grad_values = jnp.einsum(
            "gbn,bgd->nd", probs.astype(jnp.bfloat16), head_grad, preferred_element_type=jnp.float32
        )
        return (grad_query, grad_keys, grad_values)

    grad_queries, grad_keys, grad_values = lax.map(
        backward_one_head, (head_query_rows, head_gradient, log_total, keys_heads, values_heads)
    )
    return (
        grad_queries.transpose(1, 0, 2, 3).reshape(row_sizes, QUERY_HEADS, HEAD_SIZE),
        grad_keys,
        grad_values,
    )


def expert_forward(
    expert_row_set,
    expert_labels,
    entry_weight,
    down_weight,
    adapter_first,
    adapter_second,
    adapter_down_first,
    adapter_down_second,
):
    adapter_rank_width = ADAPTER_POOL * ADAPTER_RANK
    rank_entry = (
        batched_apply(expert_row_set, adapter_first) * adapter_rank_mask(expert_labels, 2)
    ).astype(jnp.bfloat16)
    gate_and_up = batched_apply(expert_row_set, entry_weight) + jnp.concatenate(
        [
            batched_apply(
                rank_entry[..., :adapter_rank_width], adapter_second[..., :EXPERT_HIDDEN]
            ),
            batched_apply(
                rank_entry[..., adapter_rank_width:], adapter_second[..., EXPERT_HIDDEN:]
            ),
        ],
        axis=-1,
    )
    hidden_middle = (
        jax.nn.silu(gate_and_up[..., :EXPERT_HIDDEN]) * gate_and_up[..., EXPERT_HIDDEN:]
    ).astype(jnp.bfloat16)
    rank_lower = (
        batched_apply(hidden_middle, adapter_down_first) * adapter_rank_mask(expert_labels, 1)
    ).astype(jnp.bfloat16)
    expert_output = (
        batched_apply(hidden_middle, down_weight) + batched_apply(rank_lower, adapter_down_second)
    ).astype(jnp.bfloat16)
    return (rank_entry, gate_and_up, hidden_middle, rank_lower, expert_output)


def expert_backward(
    gradient_output,
    expert_row_set,
    expert_labels,
    rank_entry,
    gate_and_up,
    hidden_middle,
    rank_lower,
    entry_weight,
    down_weight,
    adapter_first,
    adapter_second,
    adapter_down_first,
    adapter_down_second,
):
    adapter_rank_width = ADAPTER_POOL * ADAPTER_RANK
    gradient_down_second = batched_row_set(rank_lower, gradient_output)
    gradient_rank_lower = batched_backward(gradient_output, adapter_down_second).astype(
        jnp.bfloat16
    ) * adapter_rank_mask(expert_labels, 1)
    gradient_down_first = batched_row_set(hidden_middle, gradient_rank_lower)
    grad_hidden = batched_backward(gradient_output, down_weight) + batched_backward(
        gradient_rank_lower, adapter_down_first
    )
    gate_part = gate_and_up[..., :EXPERT_HIDDEN]
    up_part = gate_and_up[..., EXPERT_HIDDEN:]
    sigmoid_gate = jax.nn.sigmoid(gate_part)
    gradient_gate_and_up = jnp.concatenate(
        [
            grad_hidden * up_part * sigmoid_gate * (1.0 + gate_part * (1.0 - sigmoid_gate)),
            grad_hidden * gate_part * sigmoid_gate,
        ],
        axis=-1,
    ).astype(jnp.bfloat16)
    gradient_middle = jnp.concatenate(
        [
            batched_row_set(
                rank_entry[..., :adapter_rank_width], gradient_gate_and_up[..., :EXPERT_HIDDEN]
            ),
            batched_row_set(
                rank_entry[..., adapter_rank_width:], gradient_gate_and_up[..., EXPERT_HIDDEN:]
            ),
        ],
        axis=-1,
    )
    gradient_rank_entry = jnp.concatenate(
        [
            batched_backward(
                gradient_gate_and_up[..., :EXPERT_HIDDEN], adapter_second[..., :EXPERT_HIDDEN]
            ),
            batched_backward(
                gradient_gate_and_up[..., EXPERT_HIDDEN:], adapter_second[..., EXPERT_HIDDEN:]
            ),
        ],
        axis=-1,
    ).astype(jnp.bfloat16) * adapter_rank_mask(expert_labels, 2)
    gradient_adapter_first = batched_row_set(expert_row_set, gradient_rank_entry)
    gradient_row_set = (
        batched_backward(gradient_gate_and_up, entry_weight)
        + batched_backward(gradient_rank_entry, adapter_first)
    ).astype(jnp.bfloat16)
    return (
        gradient_row_set,
        gradient_adapter_first,
        gradient_middle,
        gradient_down_first,
        gradient_down_second,
    )


def local(
    layer_input,
    output_gradient,
    routes,
    sequence_adapter,
    attention_gain,
    experts_gain,
    project_weight,
    output_weight,
    router_weight,
    adapter_project_first,
    adapter_project_second,
    adapter_output_first,
    adapter_output_second,
    adapter_router_first,
    adapter_router_second,
    expert_gate_up_weight,
    expert_down_weight,
    adapter_expert_first,
    adapter_expert_second,
    adapter_expert_down_first,
    adapter_expert_down_second,
):
    shards = lax.axis_size("shard")
    token_each_device = layer_input.shape[0]
    group_token_count = token_each_device * shards
    exp_dev = expert_gate_up_weight.shape[0]
    adapter_rank_width = ADAPTER_POOL * ADAPTER_RANK
    query_width = QUERY_HEADS * HEAD_SIZE
    key_value_width = KEY_HEADS * HEAD_SIZE
    capacity = token_each_device * TOPK // EXPERT_COUNT * 5 // 4
    score_scale = HEAD_SIZE ** (-0.5)
    fetched = (
        lax.all_gather(project_weight, "shard", axis=1, tiled=True),
        lax.all_gather(output_weight, "shard", axis=0, tiled=True),
        lax.all_gather(router_weight, "shard", axis=0, tiled=True),
        lax.all_gather(adapter_project_first, "shard", axis=0, tiled=True),
        lax.all_gather(adapter_project_second, "shard", axis=1, tiled=True),
        lax.all_gather(adapter_output_first, "shard", axis=0, tiled=True),
        lax.all_gather(adapter_output_second, "shard", axis=1, tiled=True),
        lax.all_gather(adapter_router_first, "shard", axis=0, tiled=True),
        lax.all_gather(adapter_router_second, "shard", axis=1, tiled=True),
    )
    local_rows = lax.axis_index("shard") * token_each_device + jnp.arange(
        token_each_device, dtype=jnp.int32
    )
    sequence, position = token_layout(local_rows)
    key_sequence, key_position = token_layout(jnp.arange(group_token_count, dtype=jnp.int32))
    adapter = jnp.sum(
        jnp.where(
            sequence[:, None] == jnp.arange(sequence_adapter.shape[1], dtype=jnp.int32)[None, :],
            sequence_adapter,
            0,
        ),
        axis=1,
    )
    onehot = (adapter[:, None] == jnp.arange(ADAPTER_POOL, dtype=jnp.int32)[None, :]).astype(
        jnp.bfloat16
    )
    mask_one = adapter_rank_mask(onehot, 1)
    mask_three = adapter_rank_mask(onehot, 3)
    cosine_table, sine_table = rotary_table(position)
    residual = layer_input.astype(jnp.float32)
    inverse_one = lax.rsqrt(jnp.mean(residual * residual, axis=-1, keepdims=True) + EPSILON)
    normed = (residual * inverse_one * attention_gain).astype(jnp.bfloat16)
    rank_qkv = (matmul(normed, fetched[3]) * mask_three).astype(jnp.bfloat16)
    rank_extra = jnp.concatenate(
        [
            matmul(rank_qkv[:, :adapter_rank_width], fetched[4][:, :query_width]),
            matmul(
                rank_qkv[:, adapter_rank_width : 2 * adapter_rank_width],
                fetched[4][:, query_width : query_width + key_value_width],
            ),
            matmul(
                rank_qkv[:, 2 * adapter_rank_width :],
                fetched[4][:, query_width + key_value_width :],
            ),
        ],
        axis=1,
    )
    projected_rows = matmul(normed, fetched[0]) + rank_extra
    queries = rotate_halves(
        projected_rows[:, :query_width].reshape(token_each_device, QUERY_HEADS, HEAD_SIZE),
        cosine_table,
        sine_table,
    ).astype(jnp.bfloat16)
    keys_rotated = rotate_halves(
        projected_rows[:, query_width : query_width + key_value_width].reshape(
            token_each_device, KEY_HEADS, HEAD_SIZE
        ),
        cosine_table,
        sine_table,
    ).astype(jnp.bfloat16)
    value_local_rows = (
        projected_rows[:, query_width + key_value_width :]
        .reshape(token_each_device, KEY_HEADS, HEAD_SIZE)
        .astype(jnp.bfloat16)
    )
    keys_heads, values_heads = (
        lax.all_gather(keys_rotated.transpose(1, 0, 2), "shard", axis=1, tiled=True),
        lax.all_gather(value_local_rows.transpose(1, 0, 2), "shard", axis=1, tiled=True),
    )
    blocks = token_each_device // token_each_device
    query_blocks = queries.reshape(blocks, token_each_device, QUERY_HEADS, HEAD_SIZE)
    seq_blocks = sequence.reshape(blocks, token_each_device)
    pos_blocks = position.reshape(blocks, token_each_device)

    def forward_step(parts_list):
        return forward_block(
            parts_list[0],
            parts_list[1],
            parts_list[2],
            keys_heads,
            values_heads,
            key_sequence,
            key_position,
            score_scale,
        )

    mixed_blocks, log_total = lax.map(forward_step, (query_blocks, seq_blocks, pos_blocks))
    mixed = mixed_blocks.reshape(token_each_device, query_width)
    rank_out = (matmul(mixed, fetched[5]) * mask_one).astype(jnp.bfloat16)
    hidden_one = residual + matmul(mixed, fetched[1]) + matmul(rank_out, fetched[6])
    inverse_two = lax.rsqrt(jnp.mean(hidden_one * hidden_one, axis=-1, keepdims=True) + EPSILON)
    moe_in = (hidden_one * inverse_two * experts_gain).astype(jnp.bfloat16)
    rank_router = (matmul(moe_in, fetched[7]) * mask_one).astype(jnp.bfloat16)
    logits = matmul(moe_in, fetched[2]) + matmul(rank_router, fetched[8])
    choose = (
        routes[:, :, None] == jnp.arange(EXPERT_COUNT, dtype=jnp.int32)[None, None, :]
    ).astype(jnp.float32)
    picked = jnp.sum(logits[:, None, :] * choose, axis=-1)
    gate_weights = jax.nn.softmax(picked, axis=-1)
    grad_top = output_gradient.astype(jnp.float32)
    target, slot_assign = slot_layout(routes, capacity)
    slot_token = slot_assign // TOPK
    moe_ext = jnp.concatenate([moe_in, jnp.zeros((1, MODEL_WIDTH), jnp.bfloat16)], axis=0)
    tag_ext = jnp.concatenate([onehot, jnp.zeros((1, ADAPTER_POOL), jnp.bfloat16)], axis=0)
    send_rows = moe_ext[slot_token].reshape(shards, exp_dev, capacity, MODEL_WIDTH)
    send_tags = tag_ext[slot_token].reshape(shards, exp_dev, capacity, ADAPTER_POOL)
    got_rows, got_tags = (
        lax.all_to_all(send_rows, "shard", split_axis=0, concat_axis=2, tiled=True),
        lax.all_to_all(send_tags, "shard", split_axis=0, concat_axis=2, tiled=True),
    )
    expert_row_set = got_rows[0]
    expert_labels = got_tags[0]
    rank_entry, gate_and_up, hidden_middle, rank_lower, expert_output = expert_forward(
        expert_row_set,
        expert_labels,
        expert_gate_up_weight,
        expert_down_weight,
        adapter_expert_first,
        adapter_expert_second,
        adapter_expert_down_first,
        adapter_expert_down_second,
    )
    returned = lax.all_to_all(
        expert_output[None], "shard", split_axis=2, concat_axis=0, tiled=True
    ).reshape(EXPERT_COUNT * capacity, MODEL_WIDTH)
    chosen_rows = returned[target].reshape(token_each_device, TOPK, MODEL_WIDTH)
    block_out = (hidden_one + jnp.sum(gate_weights[:, :, None] * chosen_rows, axis=1)).astype(
        jnp.bfloat16
    )
    grad_gates = jnp.sum(grad_top[:, None, :] * chosen_rows, axis=-1)
    grad_ext = jnp.concatenate([grad_top, jnp.zeros((1, MODEL_WIDTH), jnp.float32)], axis=0)
    gate_ext = jnp.concatenate([gate_weights.reshape(-1), jnp.zeros((1,), jnp.float32)], axis=0)
    grad_send = (
        (grad_ext[slot_token] * gate_ext[slot_assign][:, None])
        .astype(jnp.bfloat16)
        .reshape(shards, exp_dev, capacity, MODEL_WIDTH)
    )
    gradient_output = lax.all_to_all(grad_send, "shard", split_axis=0, concat_axis=2, tiled=True)[0]
    gradient_row_set, grad_ex_in, grad_ex_mid, grad_ex_down_in, grad_ex_down_out = expert_backward(
        gradient_output,
        expert_row_set,
        expert_labels,
        rank_entry,
        gate_and_up,
        hidden_middle,
        rank_lower,
        expert_gate_up_weight,
        expert_down_weight,
        adapter_expert_first,
        adapter_expert_second,
        adapter_expert_down_first,
        adapter_expert_down_second,
    )
    grad_back = lax.all_to_all(
        gradient_row_set[None], "shard", split_axis=2, concat_axis=0, tiled=True
    ).reshape(EXPERT_COUNT * capacity, MODEL_WIDTH)
    grad_moe_in = jnp.sum(
        grad_back[target].reshape(token_each_device, TOPK, MODEL_WIDTH), axis=1, dtype=jnp.float32
    )
    weights_now = (
        lax.all_gather(project_weight, "shard", axis=1, tiled=True),
        lax.all_gather(output_weight, "shard", axis=0, tiled=True),
        lax.all_gather(router_weight, "shard", axis=0, tiled=True),
        lax.all_gather(adapter_project_first, "shard", axis=0, tiled=True),
        lax.all_gather(adapter_project_second, "shard", axis=1, tiled=True),
        lax.all_gather(adapter_output_first, "shard", axis=0, tiled=True),
        lax.all_gather(adapter_output_second, "shard", axis=1, tiled=True),
        lax.all_gather(adapter_router_first, "shard", axis=0, tiled=True),
        lax.all_gather(adapter_router_second, "shard", axis=1, tiled=True),
    )
    grad_picked = gate_weights * (
        grad_gates - jnp.sum(grad_gates * gate_weights, axis=-1, keepdims=True)
    )
    grad_logits = jnp.sum(grad_picked[:, :, None] * choose, axis=1).astype(jnp.bfloat16)
    grad_out_router_full = matmul_rows(rank_router, grad_logits)
    grad_rank_router = matmul_back(grad_logits, weights_now[8]).astype(jnp.bfloat16) * mask_one
    grad_in_router_full = matmul_rows(moe_in, grad_rank_router)
    grad_moe_in = (
        grad_moe_in
        + matmul_back(grad_logits, weights_now[2])
        + matmul_back(grad_rank_router, weights_now[7])
    )
    grad_hidden = grad_top + norm_back(grad_moe_in, hidden_one, inverse_two, experts_gain)
    grad_branch = grad_hidden.astype(jnp.bfloat16)
    grad_out_out_full = matmul_rows(rank_out, grad_branch)
    grad_rank_out = matmul_back(grad_branch, weights_now[6]).astype(jnp.bfloat16) * mask_one
    grad_in_out_full = matmul_rows(mixed, grad_rank_out)
    grad_mixed = (
        matmul_back(grad_branch, weights_now[1]) + matmul_back(grad_rank_out, weights_now[5])
    ).astype(jnp.bfloat16)

    def backward_step(totals, parts_list):
        grad_query, grad_keys, grad_values = backward_block(
            parts_list[0],
            parts_list[1],
            parts_list[2],
            parts_list[3],
            parts_list[4],
            keys_heads,
            values_heads,
            key_sequence,
            key_position,
            score_scale,
        )
        return ((totals[0] + grad_keys, totals[1] + grad_values), grad_query)

    empty_heads = jnp.zeros((KEY_HEADS, group_token_count, HEAD_SIZE), jnp.float32)
    key_totals, grad_queries = lax.scan(
        backward_step,
        (empty_heads, empty_heads),
        (
            query_blocks,
            grad_mixed.reshape(blocks, token_each_device, query_width),
            log_total,
            seq_blocks,
            pos_blocks,
        ),
    )
    key_share, value_share = (
        lax.psum_scatter(
            key_totals[0].astype(jnp.bfloat16), "shard", scatter_dimension=1, tiled=True
        ).astype(jnp.float32),
        lax.psum_scatter(
            key_totals[1].astype(jnp.bfloat16), "shard", scatter_dimension=1, tiled=True
        ).astype(jnp.float32),
    )
    grad_q_pre = rotate_halves(
        grad_queries.reshape(token_each_device, QUERY_HEADS, HEAD_SIZE), cosine_table, -sine_table
    ).reshape(token_each_device, query_width)
    grad_k_pre = rotate_halves(key_share.transpose(1, 0, 2), cosine_table, -sine_table).reshape(
        token_each_device, key_value_width
    )
    grad_v_pre = value_share.transpose(1, 0, 2).reshape(token_each_device, key_value_width)
    grad_projected = jnp.concatenate([grad_q_pre, grad_k_pre, grad_v_pre], axis=1).astype(
        jnp.bfloat16
    )
    grad_out_qkv_full = jnp.concatenate(
        [
            matmul_rows(rank_qkv[:, :adapter_rank_width], grad_projected[:, :query_width]),
            matmul_rows(
                rank_qkv[:, adapter_rank_width : 2 * adapter_rank_width],
                grad_projected[:, query_width : query_width + key_value_width],
            ),
            matmul_rows(
                rank_qkv[:, 2 * adapter_rank_width :],
                grad_projected[:, query_width + key_value_width :],
            ),
        ],
        axis=1,
    )
    grad_rank_qkv = (
        jnp.concatenate(
            [
                matmul_back(grad_projected[:, :query_width], weights_now[4][:, :query_width]),
                matmul_back(
                    grad_projected[:, query_width : query_width + key_value_width],
                    weights_now[4][:, query_width : query_width + key_value_width],
                ),
                matmul_back(
                    grad_projected[:, query_width + key_value_width :],
                    weights_now[4][:, query_width + key_value_width :],
                ),
            ],
            axis=1,
        ).astype(jnp.bfloat16)
        * mask_three
    )
    grad_in_qkv_full = matmul_rows(normed, grad_rank_qkv)
    grad_normed = matmul_back(grad_projected, weights_now[0]) + matmul_back(
        grad_rank_qkv, weights_now[3]
    )
    input_grad = (
        grad_hidden + norm_back(grad_normed, residual, inverse_one, attention_gain)
    ).astype(jnp.bfloat16)
    shares = (
        lax.psum_scatter(
            grad_in_qkv_full.astype(jnp.bfloat16), "shard", scatter_dimension=0, tiled=True
        ).astype(jnp.float32),
        lax.psum_scatter(
            grad_out_qkv_full.astype(jnp.bfloat16), "shard", scatter_dimension=1, tiled=True
        ).astype(jnp.float32),
        lax.psum_scatter(
            grad_in_out_full.astype(jnp.bfloat16), "shard", scatter_dimension=0, tiled=True
        ).astype(jnp.float32),
        lax.psum_scatter(
            grad_out_out_full.astype(jnp.bfloat16), "shard", scatter_dimension=1, tiled=True
        ).astype(jnp.float32),
        lax.psum_scatter(
            grad_in_router_full.astype(jnp.bfloat16), "shard", scatter_dimension=0, tiled=True
        ).astype(jnp.float32),
        lax.psum_scatter(
            grad_out_router_full.astype(jnp.bfloat16), "shard", scatter_dimension=1, tiled=True
        ).astype(jnp.float32),
    )
    totals = (
        lax.psum(shares[0].astype(jnp.bfloat16), "rep").astype(jnp.float32),
        lax.psum(shares[1].astype(jnp.bfloat16), "rep").astype(jnp.float32),
        lax.psum(shares[2].astype(jnp.bfloat16), "rep").astype(jnp.float32),
        lax.psum(shares[3].astype(jnp.bfloat16), "rep").astype(jnp.float32),
        lax.psum(shares[4].astype(jnp.bfloat16), "rep").astype(jnp.float32),
        lax.psum(shares[5].astype(jnp.bfloat16), "rep").astype(jnp.float32),
        lax.psum(grad_ex_in.astype(jnp.bfloat16), "rep").astype(jnp.float32),
        lax.psum(grad_ex_mid.astype(jnp.bfloat16), "rep").astype(jnp.float32),
        lax.psum(grad_ex_down_in.astype(jnp.bfloat16), "rep").astype(jnp.float32),
        lax.psum(grad_ex_down_out.astype(jnp.bfloat16), "rep").astype(jnp.float32),
    )
    return (
        block_out,
        input_grad,
        totals[0],
        totals[1],
        totals[2],
        totals[3],
        totals[4],
        totals[5],
        totals[6],
        totals[7],
        totals[8],
        totals[9],
    )


def solution(mesh):
    return jax.shard_map(
        local,
        mesh=mesh,
        in_specs=(
            P(("rep", "shard"), None),
            P(("rep", "shard"), None),
            P(("rep", "shard"), None),
            P("rep", None),
            P(),
            P(),
            P(None, "shard"),
            P("shard", None),
            P("shard", None),
            P("shard", None),
            P(None, "shard"),
            P("shard", None),
            P(None, "shard"),
            P("shard", None),
            P(None, "shard"),
            P("shard", None, None),
            P("shard", None, None),
            P("shard", None, None),
            P("shard", None, None),
            P("shard", None, None),
            P("shard", None, None),
        ),
        out_specs=(
            P(("rep", "shard"), None),
            P(("rep", "shard"), None),
            P("shard", None),
            P(None, "shard"),
            P("shard", None),
            P(None, "shard"),
            P("shard", None),
            P(None, "shard"),
            P("shard", None, None),
            P("shard", None, None),
            P("shard", None, None),
            P("shard", None, None),
        ),
        check_vma=False,
    )
```

profile of v0, /device:TPU:0, one launch (start us, length us, event | category | flops | bytes accessed | tf_op | source)
XLA Modules:
  0.0 2054.6 jit_solution(15035618540626346895)
XLA Ops:
  33.9 35.2 %all-gather.5.cloned.1.call-done = bf16[1024,2048]{1,0:T(8,128)(2,1)} async-done(((bf16[1024,1024]{1,0:T(8,128)(2,1)}), bf16[1024,2048]{1,0:T(8,128)(2,1)}) %all-gather.5.cloned.1.call-update) | async-done | bytes 4194320 | tf_op jit(solution)/shard_map/all_gather | solution.py:355
  89.1 16.7 reduce-window.6
  113.3 23.0 %scatter_custom_fusion = s32[7680]{0:T(1024)S(1)} fusion(s32[6144]{0:T(1024)S(1)} %bitcast.362, s32[6144]{0:T(1024)S(1)} %iota.55, s32[]{:T(128)} %constant.209.clone.1), kind=kCustom, calls=%fused_computation.230 | custom fusion | bytes 30724 | tf_op jit(solution)/shard_map/scatter | solution.py:120
  137.0 16.3 gather_fusion.1
  183.4 96.3 %while.50 = (s32[]{:T(128)}, bf16[8,768,2,64]{1,3,2,0:T(8,128)(2,1)}, f32[8,2,768]{2,1,0:T(2,128)}, bf16[8,1536,64]{1,2,0:T(8,128)(2,1)}, bf16[8,1536,64]{1,2,0:...) while((s32[]{:T(128)}, ...), condition=%wide.region_5.6_spmd.clone.clone, body=%wide.region_2.5_spmd.clone.sunk.clone | while | flops 637008384 | bytes 34084972 | solution.py:148
  291.5 35.2 %gather_fusion = bf16[7680,1024]{1,0:T(8,128)(2,1)} fusion(bf16[769,1024]{1,0:T(8,128)(2,1)} %concatenate.76, s32[8192]{0:T(1024)S(1)} %get-tuple-element.336), kind=kCustom, calls=%fused_computation | custom fusion | bytes 31488000 | tf_op jit(solution)/shard_map/gather | solution.py:459
  326.7 20.1 all-to-all-start
  350.3 35.0 %gather_fusion.3 = f32[7680,1024]{1,0:T(8,128)} fusion(f32[769,1024]{1,0:T(8,128)} %concatenate.80, s32[8192]{0:T(1024)S(1)} %get-tuple-element.336), kind=kCustom, calls=%fused_computation.3 | custom fusion | bytes 62945280 | tf_op jit(solution)/shard_map/gather | solution.py:488
  385.4 130.6 %all_gather.52 = bf16[64,32]{0,1:T(8,128)(2,1)S(1)} all-gather(bf16[64,16]{0,1:T(8,128)(2,1)S(1)} %copy-done.103), channel_id=1, replica_groups=mesh['rep'=16,'shard'=2] {'shard'}, dimensions={1}, use_global_device_ids=true | all-gather | bytes 6144 | tf_op jit(solution)/shard_map/all_gather | solution.py:363
  532.7 39.8 %gather_fusion.4 = f32[7680]{0:T(1024)S(1)} fusion(f32[6145]{0:T(1024)S(1)} %pad_maximum_fusion.6, s32[8192]{0:T(1024)S(1)} %copy-done.79), kind=kCustom, calls=%fused_computation.4 | custom fusion | bytes 92160 | tf_op jit(solution)/shard_map/gather | solution.py:488
  572.6 16.7 multiply_convert_fusion
  599.7 13.4 copy.216
  613.2 11.8 multiply_convert_fusion.4
  642.3 122.2 %all-to-all-done.3 = bf16[2,16,240,1024]{3,2,1,0:T(8,128)(2,1)} async-done(((bf16[2,16,240,1024]{3,2,1,0:T(8,128)(2,1)}), bf16[2,16,240,1024]{3,2,1,0:T(8,128)(2,1)}, u32[]{:S(2)}, u32[]{:S(2)}) %all-to-all-start.3) | async-done | bytes 15728672 | tf_op jit(solution)/shard_map/all_to_all | solution.py:492
  764.5 13.4 copy.225
  787.1 21.0 %fusion.162 = f32[16,480,512]{2,1,0:T(8,128)} fusion(bf16[16,480,1024]{2,1,0:T(8,128)(2,1)} %bitcast.325, bf16[16,512,1024]{2,1,0:T(8,128)(2,1)} %param.41), kind=kOutput, calls=%fused_computation.289 | convolution fusion | flops 8053063680 | bytes 48234496 | tf_op jit(solution)/shard_map/dot_general | solution.py:49
  808.2 43.1 %maximum_add_fusion = f32[16,480,1024]{2,1,0:T(8,128)} fusion(f32[16,480,512]{2,1,0:T(8,128)} %fusion.90, f32[16,480,512]{2,1,0:T(8,128)} %fusion.93, bf16[16,480,1024]{2,1,0:T(8,128)(2,1)} %bitcast.329, bf16[16,1024,1024]{2,1,0:T(8,128)(2,1)} %param.40), kind=kOutput, calls=%fused_computation.71 | convolution fusion | flops 16121856000 | bytes 112197632 | tf_op jit(solution)/shard_map/dot_general | solution.py:43
  851.3 23.5 %multiply_convert_fusion.2 = (bf16[16,480,512]{2,1,0:T(8,128)(2,1)S(1)}, bf16[16,480,512]{2,1,0:T(8,128)(2,1)}, bf16[16,480,512]{2,1,0:T(8,128)(2,1)}) fusion(f32[16,480,1024]{2,1,0:T(8,128)} %maximum_add_fusion, f32[16,480,512]{2,1,0:T(8,128)} %fusion.162, bf16[16,480,64]{1,2,0:T(8,128)(2,1)} %fusion.83, bf16[16,512,64]{1,2,0:T(8,128)(2,1)} %param.44), kind=kOutput, calls=%fused_computation.87 | convolution fusion | flops 570163200 | bytes 72810496 | tf_op jit(solution)/shard_map/dot_general | solution.py:49
  888.0 36.0 %fusion.62 = f32[16,480,1024]{2,1,0:T(8,128)} fusion(bf16[16,1024,1024]{2,1,0:T(8,128)(2,1)} %param.40, bf16[16,480,512]{2,1,0:T(8,128)(2,1)} %get-tuple-element.308, bf16[16,480,512]{2,1,0:T(8,128)(2,1)} %copy-done.8), kind=kOutput, calls=%fused_computation.82 | convolution fusion | flops 16137584640 | bytes 80740352 | tf_op jit(solution)/shard_map/dot_general | solution.py:49
  924.0 18.5 fusion.61
  942.5 34.8 %copy.227 = bf16[1,16,480,1024]{3,1,0,2:T(8,128)(2,1)} copy(bf16[1,16,480,1024]{3,2,1,0:T(8,128)(2,1)} %fusion.61) | data formatting | bytes 31457280 | tf_op jit(solution)/shard_map/broadcast_in_dim | solution.py:509
  992.9 21.8 %fusion.161 = f32[16,480,1024]{2,1,0:T(8,128)} fusion(bf16[16,480,512]{2,1,0:T(8,128)(2,1)} %get-tuple-element.309, bf16[16,512,1024]{2,1,0:T(8,128)(2,1)} %param.41), kind=kOutput, calls=%fused_computation.288 | convolution fusion | flops 8053063680 | bytes 56098816 | tf_op jit(solution)/shard_map/dot_general | solution.py:43
  1014.7 11.4 fusion.60
  1026.2 25.3 %copy.222 = bf16[1,16,480,1024]{3,1,0,2:T(8,128)(2,1)} copy(bf16[1,16,480,1024]{3,2,1,0:T(8,128)(2,1)S(1)} %fusion.60) | data formatting | bytes 31457280 | tf_op jit(solution)/shard_map/broadcast_in_dim | solution.py:478
  1051.5 100.0 %all-to-all-done.4 = bf16[1,16,480,1024]{3,1,0,2:T(8,128)(2,1)} async-done(((bf16[1,16,480,1024]{3,1,0,2:T(8,128)(2,1)}), bf16[1,16,480,1024]{3,1,0,2:T(8,128)(2,1)}, u32[]{:S(2)}, u32[]{:S(2)}) %all-to-all-start.4) | async-done | bytes 15728672 | tf_op jit(solution)/shard_map/all_to_all | solution.py:508
  1164.5 18.1 copy.228
  1182.5 38.4 %gather_fusion.5 = bf16[6144,1024]{1,0:T(8,128)(2,1)} fusion(bf16[7680,1024]{1,0:T(8,128)(2,1)} %bitcast.322, s32[6144]{0:T(1024)S(1)} %broadcast_clamp_fusion), kind=kCustom, calls=%fused_computation.5 | custom fusion | bytes 25190400 | tf_op jit(solution)/shard_map/gather | solution.py:512
  1220.9 11.8 convert_reduce_fusion
  1232.7 92.3 %all-to-all-done.2 = bf16[1,16,480,1024]{3,1,0,2:T(8,128)(2,1)} async-done(((bf16[1,16,480,1024]{3,1,0,2:T(8,128)(2,1)}), bf16[1,16,480,1024]{3,1,0,2:T(8,128)(2,1)}, u32[]{:S(2)}, u32[]{:S(2)}) %all-to-all-start.2) | async-done | bytes 15728672 | tf_op jit(solution)/shard_map/all_to_all | solution.py:477
  1324.9 17.8 copy.223
  1342.8 38.4 %gather_fusion.2 = bf16[6144,1024]{1,0:T(8,128)(2,1)} fusion(bf16[7680,1024]{1,0:T(8,128)(2,1)} %bitcast.321, s32[6144]{0:T(1024)S(1)} %broadcast_clamp_fusion), kind=kCustom, calls=%fused_computation.2 | custom fusion | bytes 25190400 | tf_op jit(solution)/shard_map/gather | solution.py:480
  1381.2 14.4 fusion.59
  1412.1 280.4 %while.51 = (s32[]{:T(128)}, f32[8,768,2,64]{1,3,2,0:T(8,128)}, bf16[8,1536,64]{1,2,0:T(8,128)(2,1)}, bf16[8,1536,64]{1,2,0:T(8,128)(2,1)}, bf16[8,1536,64]{1,2,...) while((s32[]{:T(128)}, f32[8,768,2,64]{1,3,2,0:T(8,128)}, ...), condition=%wide.region_22.23_spmd.clone.clone, body=%wide.region_20.22_spmd.clone.sunk.clone | while | flops 1536096768 | bytes 151247552 | solution.py:205
  1425.4 9.8 fusion.282
  1460.5 9.8 fusion.282
  1495.5 9.8 fusion.282
  1530.6 9.8 fusion.282
  1565.6 9.8 fusion.282
  1600.6 9.8 fusion.282
  1635.7 9.8 fusion.282
  1670.7 9.8 fusion.282
  1708.5 13.9 convolution_convert_fusion
  1773.1 12.5 reduce-scatter.21.cloned.1.call-done
  1785.6 14.3 reduce-scatter.15.cloned.1.call-done
  1799.9 16.1 reduce-scatter.13.cloned.1.call-done
  1816.0 12.4 reduce-scatter.23.cloned.1.call-done
  1828.4 34.2 %psum.75 = bf16[64,16]{0,1:T(8,128)(2,1)S(1)} all-reduce(bf16[64,16]{0,1:T(8,128)(2,1)} %reduce-scatter.23.cloned.1.call-done), channel_id=1, replica_groups=mesh['rep'=16,'shard'=2] {'rep'}, use_global_device_ids=true, to_apply=%region_37.38 | all-reduce | flops 1024 | bytes 4096 | tf_op jit(solution)/shard_map/psum | solution.py:655
  1873.7 157.2 %all-reduce.6.cloned.1.call-done = (bf16[512,192]{0,1:T(8,128)(2,1)}, bf16[64,1024]{1,0:T(8,128)(2,1)}, bf16[512,64]{0,1:T(8,128)(2,1)}, bf16[64,512]{1,0:T(8,12...) async-done(((bf16[512,192]{0,1:T(8,128)(2,1)}, ...) | async-done | bytes 9961488 | tf_op jit(solution)/shard_map/psum | solution.py:650
  (504 shorter events, 603.5 us)
Async XLA Ops:
  7.2 770.7 %copy-start = (bf16[16,64,1024]{2,1,0:T(8,128)(2,1)S(1)}, bf16[16,64,1024]{2,1,0:T(8,128)(2,1)}, u32[]{:S(2)}) copy-start(bf16[16,64,1024]{2,1,0:T(8,128)(2,1)} %param.45) | copy-start | bytes 6291460
  7.2 19.0 copy-start.101
  7.2 61.9 %all-gather.5.cloned.1.call-start = ((), (), s32[]{:S(2)}) async-start(), calls=%async_computation.13 | async-start | bytes 6291456 | tf_op jit(solution)/shard_map/all_gather | solution.py:355
  7.9 175.4 %all-gather.9.cloned.1.call-start = ((), (), s32[]{:S(2)}) async-start(), calls=%async_computation.15 | async-start | bytes 2359296 | tf_op jit(solution)/shard_map/all_gather | solution.py:421
  15.4 16.2 copy-start.30
  25.1 44.0 %copy-start.96 = (f32[768]{0:T(1024)}, f32[768]{0:T(1024)S(1)}, u32[]{:S(2)}) copy-start(f32[768]{0:T(1024)S(1)} %add_rsqrt_fusion.1) | copy-start | bytes 9220
  26.2 153.5 %copy-start.28 = (f32[768,32]{0,1:T(8,128)}, f32[768,32]{0,1:T(8,128)S(1)}, u32[]{:S(2)}) copy-start(f32[768,32]{0,1:T(8,128)S(1)} %get-tuple-element.324) | copy-start | bytes 294916
  26.2 501.3 %copy-start.21 = (bf16[768,4,16]{0,2,1:T(8,128)(2,1)}, bf16[768,4,16]{0,2,1:T(8,128)(2,1)S(1)}, u32[]{:S(2)}) copy-start(bf16[768,4,16]{0,2,1:T(8,128)(2,1)S(1)} %broadcast_in_dim.99) | copy-start | bytes 294916
  86.7 96.7 %all-gather.7.cloned.1.call-start = ((), (), s32[]{:S(2)}) async-start(), calls=%async_computation.14 | async-start | bytes 2359296 | tf_op jit(solution)/shard_map/all_gather | solution.py:422
  113.3 40.0 %copy-start.82 = (s32[6144,1]{0,1:T(1,128)}, s32[6144,1]{0,1:T(1,128)S(1)}, u32[]{:S(2)}) copy-start(s32[6144,1]{0,1:T(1,128)S(1)} %compare_select_fusion) | copy-start | bytes 73732
  156.0 170.7 %all-to-all-start.1 = ((bf16[2,16,240,4]{2,1,3,0:T(8,128)(2,1)}), bf16[2,16,240,4]{2,1,3,0:T(8,128)(2,1)}, u32[]{:S(2)}, u32[]{:S(2)}) async-start(bf16[2,16,240,4]{2,1,3,0:T(8,128)(2,1)} %copy.218), calls=%async_computation.1 | async-start | bytes 131072 | tf_op jit(solution)/shard_map/all_to_all | solution.py:463
  159.9 122.2 %all-gather.11.cloned.1.call-start = ((), (), s32[]{:S(2)}) async-start(), calls=%async_computation.16 | async-start | bytes 3145728 | tf_op jit(solution)/shard_map/all_gather | solution.py:356
  166.7 113.5 %copy-start.43 = (bf16[1024,64]{0,1:T(8,128)(2,1)}, bf16[1024,64]{0,1:T(8,128)(2,1)S(1)}, u32[]{:S(2)}) copy-start(bf16[1024,64]{0,1:T(8,128)(2,1)S(1)} %all_gather.48) | copy-start | bytes 393220
  171.9 114.2 %copy-start.39 = (bf16[64,1024]{1,0:T(8,128)(2,1)}, bf16[64,1024]{1,0:T(8,128)(2,1)S(1)}, u32[]{:S(2)}) copy-start(bf16[64,1024]{1,0:T(8,128)(2,1)S(1)} %all_gather.49) | copy-start | bytes 393220
  326.7 262.6 %all-to-all-start = ((bf16[2,16,240,1024]{3,2,1,0:T(8,128)(2,1)}), bf16[2,16,240,1024]{3,2,1,0:T(8,128)(2,1)}, u32[]{:S(2)}, u32[]{:S(2)}) async-start(bf16[2,16,240,1024]{3,2,1,0:T(8,128)(2,1)} %bitcast.327), calls=%async_computation | async-start | bytes 31457280 | tf_op jit(solution)/shard_map/all_to_all | solution.py:462
  350.3 35.0 %copy-start.103 = (bf16[64,16]{0,1:T(8,128)(2,1)S(1)}, bf16[64,16]{0,1:T(8,128)(2,1)}, u32[]{:S(2)}) copy-start(bf16[64,16]{0,1:T(8,128)(2,1)} %param.39) | copy-start | bytes 6148
  350.3 165.7 %copy-start.98 = (bf16[512,32]{0,1:T(8,128)(2,1)S(1)}, bf16[512,32]{0,1:T(8,128)(2,1)}, u32[]{:S(2)}) copy-start(bf16[512,32]{0,1:T(8,128)(2,1)} %param.33) | copy-start | bytes 98308
  350.3 170.3 %copy-start.90 = (bf16[512,64]{0,1:T(8,128)(2,1)S(1)}, bf16[512,64]{0,1:T(8,128)(2,1)}, u32[]{:S(2)}) copy-start(bf16[512,64]{0,1:T(8,128)(2,1)} %param.38) | copy-start | bytes 196612
  385.3 144.9 %copy-start.73 = (s32[768,8]{0,1:T(8,128)S(1)}, s32[768,8]{0,1:T(8,128)}, u32[]{:S(2)}) copy-start(s32[768,8]{0,1:T(8,128)} %param.27) | copy-start | bytes 73732
  385.3 147.3 %copy-start.79 = (s32[8192]{0:T(1024)S(1)}, s32[8192]{0:T(1024)}, u32[]{:S(2)}) copy-start(s32[8192]{0:T(1024)} %get-tuple-element.335) | copy-start | bytes 98308
  516.0 14.4 copy-start.84
  589.3 175.3 %all-to-all-start.3 = ((bf16[2,16,240,1024]{3,2,1,0:T(8,128)(2,1)}), bf16[2,16,240,1024]{3,2,1,0:T(8,128)(2,1)}, u32[]{:S(2)}, u32[]{:S(2)}) async-start(bf16[2,16,240,1024]{3,2,1,0:T(8,128)(2,1)} %multiply_convert_fusion), calls=%async_computation.3 | async-start | bytes 31457280 | tf_op jit(solution)/shard_map/all_to_all | solution.py:492
  613.2 310.7 %copy-start.16 = (bf16[16,480,4,16]{1,3,2,0:T(8,128)(2,1)}, bf16[16,480,4,16]{1,3,2,0:T(8,128)(2,1)S(1)}, u32[]{:S(2)}) copy-start(bf16[16,480,4,16]{1,3,2,0:T(8,128)(2,1)S(1)} %broadcast_in_dim.113) | copy-start | bytes 2949124
  977.2 174.3 %all-to-all-start.4 = ((bf16[1,16,480,1024]{3,1,0,2:T(8,128)(2,1)}), bf16[1,16,480,1024]{3,1,0,2:T(8,128)(2,1)}, u32[]{:S(2)}, u32[]{:S(2)}) async-start(bf16[1,16,480,1024]{3,1,0,2:T(8,128)(2,1)} %copy.227), calls=%async_computation.4 | async-start | bytes 31457280 | tf_op jit(solution)/shard_map/all_to_all | solution.py:508
  992.9 21.8 %copy-start.12 = (bf16[16,480,64]{1,2,0:T(8,128)(2,1)}, bf16[16,480,64]{1,2,0:T(8,128)(2,1)S(1)}, u32[]{:S(2)}) copy-start(bf16[16,480,64]{1,2,0:T(8,128)(2,1)S(1)} %multiply_convert_fusion.6) | copy-start | bytes 2949124
  1151.5 173.4 %all-to-all-start.2 = ((bf16[1,16,480,1024]{3,1,0,2:T(8,128)(2,1)}), bf16[1,16,480,1024]{3,1,0,2:T(8,128)(2,1)}, u32[]{:S(2)}, u32[]{:S(2)}) async-start(bf16[1,16,480,1024]{3,1,0,2:T(8,128)(2,1)} %copy.222), calls=%async_computation.2 | async-start | bytes 31457280 | tf_op jit(solution)/shard_map/all_to_all | solution.py:477
  1160.9 576.8 %reduce-scatter.9.cloned.1.call-start = ((), (), s32[]{:S(2)}) async-start(), calls=%async_computation.17 | async-start | bytes 2359296 | tf_op jit(solution)/shard_map/reduce_scatter | solution.py:574
  1342.8 38.4 %copy-start.25 = (f32[768,8]{1,0:T(8,128)S(1)}, f32[768,8]{1,0:T(8,128)}, u32[]{:S(2)}) copy-start(f32[768,8]{1,0:T(8,128)} %copy-done.24) | copy-start | bytes 73732
  1381.2 14.6 copy-start.58
  1381.2 14.6 copy-start.81
  1381.2 14.5 copy-start.95
  1381.2 14.6 copy-start.74
  1381.2 14.7 copy-start.22
  1381.2 14.7 copy-start.85
  1381.2 14.9 copy-start.46
  1692.5 54.4 %reduce-scatter.11.cloned.1.call-start = ((), (), s32[]{:S(2)}) async-start(), calls=%async_computation.18 | async-start | bytes 2359296 | tf_op jit(solution)/shard_map/reduce_scatter | solution.py:577
  1708.4 14.0 copy-start.29
  1708.4 14.0 copy-start.56
  1708.4 62.0 %reduce-scatter.17.cloned.1.call-start = ((), (), s32[]{:S(2)}) async-start(), calls=%async_computation.21 | async-start | bytes 196608 | tf_op jit(solution)/shard_map/reduce_scatter | solution.py:636
  1708.5 13.9 copy-start.27
  1732.6 40.5 %reduce-scatter.19.cloned.1.call-start = ((), (), s32[]{:S(2)}) async-start(), calls=%async_computation.22 | async-start | bytes 196608 | tf_op jit(solution)/shard_map/reduce_scatter | solution.py:639
  1735.1 50.5 %reduce-scatter.21.cloned.1.call-start = ((), (), s32[]{:S(2)}) async-start(), calls=%async_computation.23 | async-start | bytes 196608 | tf_op jit(solution)/shard_map/reduce_scatter | solution.py:642
  1737.7 62.3 %reduce-scatter.15.cloned.1.call-start = ((), (), s32[]{:S(2)}) async-start(), calls=%async_computation.20 | async-start | bytes 393216 | tf_op jit(solution)/shard_map/reduce_scatter | solution.py:633
  1739.3 15.5 copy-start.18
  1750.2 65.8 %reduce-scatter.13.cloned.1.call-start = ((), (), s32[]{:S(2)}) async-start(), calls=%async_computation.19 | async-start | bytes 589824 | tf_op jit(solution)/shard_map/reduce_scatter | solution.py:630
  1754.8 73.5 %reduce-scatter.23.cloned.1.call-start = ((), (), s32[]{:S(2)}) async-start(), calls=%async_computation.24 | async-start | bytes 12288 | tf_op jit(solution)/shard_map/reduce_scatter | solution.py:645
  1767.5 263.3 %all-reduce.6.cloned.1.call-start = ((), (), s32[]{:S(2)}) async-start(), calls=%async_computation.25 | async-start | bytes 19922944 | tf_op jit(solution)/shard_map/psum | solution.py:650
  1816.0 47.2 %copy-start.19 = (bf16[768,8,64]{0,2,1:T(8,128)(2,1)S(1)}, bf16[768,8,64]{0,2,1:T(8,128)(2,1)}, u32[]{:S(2)}) copy-start(bf16[768,8,64]{0,2,1:T(8,128)(2,1)} %copy-done.18) | copy-start | bytes 2359300
  (88 other events, 487.1 us)
Sparse Core Ops, SparseCore 0:
  9.6 59.4 all-gather.4
  86.8 27.2 all-gather.8
  116.2 27.2 all-gather.6
  161.9 34.5 all-gather.10
  1692.7 25.9 reduce-scatter.8
  1720.9 26.0 reduce-scatter.10
  1749.8 10.2 reduce-scatter.16
  1762.8 10.2 reduce-scatter.18
  1775.3 10.2 reduce-scatter.20
  1788.2 11.6 reduce-scatter.14
  1802.8 13.1 reduce-scatter.12
  1818.6 9.7 reduce-scatter.22
  1833.9 196.9 all-reduce.5
where the time goes:
time: 2070 us; the launch traced here: 2050 us
  matrix products  581 us (28%)
  waiting for transfers between devices  573 us (28%)
  local copies, waits for them, and re-layouts  399 us (19%)
  other arithmetic  234 us (11%)
  blocking collectives  199 us (10%)
  starting transfers between devices  52.8 us (3%)
    psum x1, waiting for transfers between devices, local(): lax.psum(shares[0].astype(jnp.bfloat16), 'rep').astype(jnp.float32)  157 us
    all_gather x1, blocking collectives, local(): lax.all_gather(adapter_router_second, 'shard', axis=1, tiled=True)  131 us
    all_to_all x1, waiting for transfers between devices, local(): lax.all_to_all(grad_send, 'shard', split_axis=0, concat_axis=2, tiled=True)  122 us
    dot_general x7, matrix products, batched_backward(): lax.dot_general(left_side, right_side, (((2,), (2,)), ((0,), (0,))), pref...  121 us
    dot_general x7, matrix products, batched_apply(): lax.dot_general(left_side, right_side, (((2,), (1,)), ((0,), (0,))), pref...  112 us
    all_to_all x1, waiting for transfers between devices, local(): lax.all_to_all(gradient_row_set[None], 'shard', split_axis=2, concat_axis...  100 us
    all_to_all x1, waiting for transfers between devices, local(): lax.all_to_all(expert_output[None], 'shard', split_axis=2, concat_axis=0,...  92.3 us
    convert_element_type x8, other arithmetic, backward_one_head(): grad_scores = (probs * (grad_probs - delta_row)).astype(jnp.bfloat16)  78.5 us
  transfers between devices with their start and end apart: 18, of which 11 were waited for; matrix products, arithmetic and copies ran while one was open for 29% of the time, Pallas kernels for 0%

commit v1 on v0

v1 whole, which is shorter than its diff:
```python
import functools
import math

import jax
import jax.numpy as jnp
from jax import lax
from jax.experimental import pallas as pl
from jax.experimental.pallas import tpu as pltpu
from jax.sharding import PartitionSpec as P

MODEL_WIDTH = 1024
QUERY_HEADS = 16
KEY_HEADS = 8
HEAD_SIZE = 64
EXPERT_COUNT = 32
EXPERT_HIDDEN = 512
TOPK = 8
ADAPTER_RANK = 16
ADAPTER_POOL = 4
PROMPT = 1024
CONT_LEN = 512


EPSILON = 1e-06
THETA = 10000.0
NEGATIVE = -1e30
F32, BF16 = jnp.float32, jnp.bfloat16


def dot_nn(a, b):
    return lax.dot_general(a, b, (((1,), (0,)), ((), ())), preferred_element_type=F32)


def dot_nt(a, b):
    return lax.dot_general(a, b, (((1,), (1,)), ((), ())), preferred_element_type=F32)


def dot_tn(a, b):
    return lax.dot_general(a, b, (((0,), (0,)), ((), ())), preferred_element_type=F32)


def expert_kernel(
    carry_acc, carry_grad,
    rows_ref, grad_ref, slot_ref, gate_ref, label_ref,
    entry_ref, down_ref, first_ref, second_ref, down_first_ref, down_second_ref,
    *refs,
):
    refs = list(refs)
    if carry_acc:
        out_in, back_in = refs[0], refs[1]
        refs = refs[2:]
    if carry_grad:
        lora_in = refs[0]
        refs = refs[1:]
    out_ref, back_ref, dgate_ref, lora_ref = refs[:4]
    x_s, dy_s, hid_s, fg_s, fu_s, dgu_s, out_s, back_s, yg_s, dx_s = refs[4:]
    cap = x_s.shape[0]
    tokens = rows_ref.shape[0]
    width = rows_ref.shape[1]
    hidden = down_ref.shape[1]
    rank = ADAPTER_POOL * ADAPTER_RANK
    e = pl.program_id(1)

    @pl.when(e == 0)
    def _():
        if carry_acc:
            out_s[...] = out_in[...]
            back_s[...] = back_in[...]
        else:
            out_s[...] = jnp.zeros_like(out_s)
            back_s[...] = jnp.zeros_like(back_s)

    slots = slot_ref[0, 0]
    gates = gate_ref[0, 0]
    hit = slots == lax.broadcasted_iota(jnp.int32, (cap, tokens), 0)
    pick32 = hit.astype(F32)
    pick = pick32.astype(BF16)
    gate_col = jnp.sum(pick32 * gates, axis=1, keepdims=True)
    label_col = jnp.sum(pick32 * label_ref[0], axis=1, keepdims=True)
    lane = lax.broadcasted_iota(jnp.int32, (cap, 2 * rank), 1)
    lane_label = ((lane // ADAPTER_RANK) % ADAPTER_POOL).astype(F32)
    mask2 = (lane_label == label_col).astype(F32)
    mask1 = mask2[:, :rank]

    x_s[...] = dot_nn(pick, rows_ref[...]).astype(BF16)
    x = x_s[...]
    ue = (dot_nn(x, first_ref[0]) * mask2).astype(BF16)
    ue0, ue1 = ue[:, :rank], ue[:, rank:]
    step = 256
    for n in range(0, hidden, step):
        g = dot_nn(x, entry_ref[0, :, n : n + step]) + dot_nn(ue0, second_ref[0, :, n : n + step])
        u = dot_nn(x, entry_ref[0, :, hidden + n : hidden + n + step]) + dot_nn(
            ue1, second_ref[0, :, hidden + n : hidden + n + step]
        )
        sig = 1.0 / (1.0 + jnp.exp(-g))
        silu = g * sig
        hid_s[:, n : n + step] = (silu * u).astype(BF16)
        fg_s[:, n : n + step] = u * sig * (1.0 + g * (1.0 - sig))
        fu_s[:, n : n + step] = silu
    hid = hid_s[...]
    ud = (dot_nn(hid, down_first_ref[0]) * mask1).astype(BF16)
    dcol = jnp.zeros((cap, 1), F32)
    for n in range(0, width, step):
        cols = slice(n, n + step)
        y = (dot_nn(hid, down_ref[0, :, cols]) + dot_nn(ud, down_second_ref[0, :, cols])).astype(BF16)
        y32 = y.astype(F32)
        gy = dot_nn(pick, grad_ref[:, cols])
        dcol = dcol + jnp.sum(gy * y32, axis=1, keepdims=True)
        dy_s[:, cols] = (gate_col * gy).astype(BF16)
        yg_s[:, cols] = (gate_col * y32).astype(BF16)
    dgate_ref[0, 0] = jnp.sum(pick32 * dcol, axis=0, keepdims=True)
    dy = dy_s[...]
    dud = (dot_nt(dy, down_second_ref[0]) * mask1).astype(BF16)
    for n in range(0, hidden, step):
        dh = dot_nt(dy, down_ref[0, n : n + step, :]) + dot_nt(dud, down_first_ref[0, n : n + step, :])
        dgu_s[:, n : n + step] = (dh * fg_s[:, n : n + step]).astype(BF16)
        dgu_s[:, hidden + n : hidden + n + step] = (dh * fu_s[:, n : n + step]).astype(BF16)
    dgu = dgu_s[...]
    dg, du = dgu[:, :hidden], dgu[:, hidden:]
    due = (
        jnp.concatenate(
            [dot_nt(dg, second_ref[0, :, :hidden]), dot_nt(du, second_ref[0, :, hidden:])], axis=1
        )
        * mask2
    ).astype(BF16)
    for n in range(0, width, step):
        cols = slice(n, n + step)
        dx = dot_nt(dgu, entry_ref[0, cols, :]) + dot_nt(due, first_ref[0, cols, :])
        dx_s[:, cols] = dx.astype(BF16)
    for n in range(0, width, step):
        cols = slice(n, n + step)
        out_s[:, cols] += dot_tn(pick, yg_s[:, cols])
        back_s[:, cols] += dot_tn(pick, dx_s[:, cols])

    def put(lo, hi, val, cols=slice(None)):
        if carry_grad:
            val = val + lora_in[0, lo:hi, cols]
        lora_ref[0, lo:hi, cols] = val.astype(lora_ref.dtype)

    put(0, 2 * rank, dot_tn(due, x))
    put(2 * rank, 3 * rank, dot_tn(ue0, dg), slice(0, hidden))
    put(2 * rank, 3 * rank, dot_tn(ue1, du), slice(hidden, 2 * hidden))
    put(3 * rank, 4 * rank, dot_tn(ud, dy))
    down_t = dot_tn(dud, hid)
    half = rank // 2
    put(4 * rank, 4 * rank + half, down_t[:half], slice(0, hidden))
    put(4 * rank, 4 * rank + half, down_t[half:], slice(hidden, 2 * hidden))

    @pl.when(e == pl.num_programs(1) - 1)
    def _():
        out_ref[...] = out_s[...].astype(out_ref.dtype)
        back_ref[...] = back_s[...].astype(back_ref.dtype)


def experts(rows, grads, slots, gates, labels, weights, cap, first, count, acc=None, lora=None, acc_type=F32, lora_type=F32):
    entry, down, a_first, a_second, d_first, d_second = weights
    blocks = slots.shape[0]
    tokens, width = rows.shape[0] // blocks, rows.shape[1]
    hidden = down.shape[1]
    rank = ADAPTER_POOL * ADAPTER_RANK
    pack = 4 * rank + rank // 2
    at_block = lambda b, e: (b, 0)
    at_expert = lambda b, e: (first + e, 0, 0)
    per = lambda b, e: (b, first + e, 0, 0)
    in_specs = [
        pl.BlockSpec((tokens, width), at_block),
        pl.BlockSpec((tokens, width), at_block),
        pl.BlockSpec((1, 1, 1, tokens), per),
        pl.BlockSpec((1, 1, 1, tokens), per),
        pl.BlockSpec((1, 1, tokens), lambda b, e: (b, 0, 0)),
    ] + [pl.BlockSpec((1,) + w.shape[1:], at_expert) for w in weights]
    args = [rows, grads, slots, gates, labels, *weights]
    if acc is not None:
        in_specs += [pl.BlockSpec((tokens, width), at_block)] * 2
        args += list(acc)
    if lora is not None:
        in_specs += [pl.BlockSpec((1, pack, width), lambda b, e: (b * count + e, 0, 0))]
        args += [lora]
    macs = cap * (width * 2 * hidden * 2 + hidden * width * 2 + 3 * (3 * width * 2 * rank)) + 4 * cap * tokens * width
    return pl.pallas_call(
        functools.partial(expert_kernel, acc is not None, lora is not None),
        grid=(blocks, count),
        in_specs=in_specs,
        out_specs=[
            pl.BlockSpec((tokens, width), at_block),
            pl.BlockSpec((tokens, width), at_block),
            pl.BlockSpec((1, 1, 1, tokens), lambda b, e: (b, e, 0, 0)),
            pl.BlockSpec((1, pack, width), lambda b, e: (b * count + e, 0, 0)),
        ],
        out_shape=[
            jax.ShapeDtypeStruct(rows.shape, acc_type),
            jax.ShapeDtypeStruct(rows.shape, acc_type),
            jax.ShapeDtypeStruct((blocks, count, 1, tokens), F32),
            jax.ShapeDtypeStruct((blocks * count, pack, width), lora_type),
        ],
        scratch_shapes=[
            pltpu.VMEM((cap, width), BF16),
            pltpu.VMEM((cap, width), BF16),
            pltpu.VMEM((cap, hidden), BF16),
            pltpu.VMEM((cap, hidden), F32),
            pltpu.VMEM((cap, hidden), F32),
            pltpu.VMEM((cap, 2 * hidden), BF16),
            pltpu.VMEM((tokens, width), F32),
            pltpu.VMEM((tokens, width), F32),
            pltpu.VMEM((cap, width), BF16),
            pltpu.VMEM((cap, width), BF16),
        ],
        compiler_params=pltpu.CompilerParams(vmem_limit_bytes=58 * 1024 * 1024),
        cost_estimate=pl.CostEstimate(
            flops=2 * macs * blocks * count, transcendentals=cap * hidden * blocks * count,
            bytes_accessed=blocks * count * 4_000_000,
        ),
        name="experts",
    )(*args)


def split_heads(pair, low):
    zero = jnp.zeros_like(pair)
    return jnp.concatenate([jnp.where(low, pair, zero), jnp.where(low, zero, pair)], axis=0)


def attend_kernel(tile, place_ref, q_ref, k_ref, v_ref, pk_ref, pv_ref, o_ref, total_ref):
    tokens = q_ref.shape[0]
    before = pk_ref.shape[0]
    place = place_ref[0]
    low = lax.broadcasted_iota(jnp.int32, (tile, 128), 1) < 64

    def tile_out(i, with_prior):
        q2 = split_heads(q_ref[i * tile : (i + 1) * tile, :], low)
        keys = (i + 1) * tile
        own = dot_nt(q2, k_ref[:keys, :])
        row = lax.broadcasted_iota(jnp.int32, (2 * tile, tile), 0) % tile
        col = lax.broadcasted_iota(jnp.int32, (2 * tile, tile), 1)
        diag = jnp.where(col <= row, own[:, i * tile :], NEGATIVE)
        parts = [diag] if i == 0 else [own[:, : i * tile], diag]
        vals = [v_ref[i * tile : keys, :]] if i == 0 else [v_ref[: i * tile, :], v_ref[i * tile : keys, :]]
        if with_prior:
            prior = dot_nt(q2, pk_ref[...])
            if before > tokens:
                seen = lax.broadcasted_iota(jnp.int32, (2 * tile, before), 1) < place * tokens
                prior = jnp.where(seen, prior, NEGATIVE)
            parts.append(prior)
            vals.append(pv_ref[...])
        peak = functools.reduce(jnp.maximum, [jnp.max(p, axis=1, keepdims=True) for p in parts])
        total = jnp.zeros((2 * tile, 1), F32)
        mix = jnp.zeros((2 * tile, 128), F32)
        for p, v in zip(parts, vals):
            w = jnp.exp(p - peak)
            total = total + jnp.sum(w, axis=1, keepdims=True)
            mix = mix + dot_nn(w.astype(BF16), v)
        mix = mix / total
        o_ref[i * tile : (i + 1) * tile, :] = jnp.where(low, mix[:tile], mix[tile:]).astype(BF16)
        logs = jnp.broadcast_to(peak + jnp.log(total), (2 * tile, 128)).T
        total_ref[0, 0:1, i * tile : (i + 1) * tile] = logs[0:1, :tile]
        total_ref[0, 1:2, i * tile : (i + 1) * tile] = logs[0:1, tile:]

    for i in range(tokens // tile):
        @pl.when(place > 0)
        def _():
            tile_out(i, True)

        @pl.when(place == 0)
        def _():
            tile_out(i, False)


def attend(place, q, kd, vd, pkd, pvd, tile):
    tokens, width = q.shape
    before = pkd.shape[0]
    pairs = width // 128
    at = lambda n, p: (0, n)
    return pl.pallas_call(
        functools.partial(attend_kernel, tile),
        grid_spec=pltpu.PrefetchScalarGridSpec(
            num_scalar_prefetch=1,
            grid=(pairs,),
            in_specs=[pl.BlockSpec((tokens, 128), at)] * 3 + [pl.BlockSpec((before, 128), at)] * 2,
            out_specs=[
                pl.BlockSpec((tokens, 128), at),
                pl.BlockSpec((1, 2, tokens), lambda n, p: (n, 0, 0)),
            ],
        ),
        out_shape=[
            jax.ShapeDtypeStruct((tokens, width), BF16),
            jax.ShapeDtypeStruct((pairs, 2, tokens), F32),
        ],
        compiler_params=pltpu.CompilerParams(vmem_limit_bytes=48 * 1024 * 1024),
        cost_estimate=pl.CostEstimate(
            flops=4 * width * tokens * (tokens + before) * 2, transcendentals=0, bytes_accessed=8 * tokens * width
        ),
        name="attend",
    )(place, q, kd, vd, pkd, pvd)


def attend_back_kernel(
    tile, place_ref, q_ref, do_ref, total_ref, delta_ref, k_ref, v_ref, pk_ref, pv_ref,
    dq_ref, dk_ref, dv_ref, dpk_ref, dpv_ref, dk_s, dv_s, dpk_s, dpv_s, dq_s,
):
    tokens = q_ref.shape[0]
    before = pk_ref.shape[0]
    place = place_ref[0]
    tiles = tokens // tile
    low = lax.broadcasted_iota(jnp.int32, (tile, 128), 1) < 64
    dk_s[...] = jnp.zeros_like(dk_s)
    dv_s[...] = jnp.zeros_like(dv_s)
    dpk_s[...] = jnp.zeros_like(dpk_s)
    dpv_s[...] = jnp.zeros_like(dpv_s)

    def block(q2, do2, logs, delta, k, v, seen, dk_acc, dv_acc, rows, first):
        s = dot_nt(k, q2)
        if seen is not None:
            s = jnp.where(seen, s, NEGATIVE)
        p = jnp.exp(s - logs)
        dp = dot_nt(v, do2)
        ds = (p * (dp - delta)).astype(BF16)
        dv_acc[rows, :] += dot_nn(p.astype(BF16), do2)
        dk_acc[rows, :] += dot_nn(ds, q2)
        dq = dot_tn(ds, k)
        if first:
            dq_s[...] = dq
        else:
            dq_s[...] += dq

    for i in range(tiles):
        here = slice(i * tile, (i + 1) * tile)
        q2 = split_heads(q_ref[here, :], low)
        do2 = split_heads(do_ref[here, :], low)
        logs = jnp.concatenate([total_ref[0, 0:1, here], total_ref[0, 1:2, here]], axis=1)
        delta = jnp.concatenate([delta_ref[0, 0:1, here], delta_ref[0, 1:2, here]], axis=1)
        row = lax.broadcasted_iota(jnp.int32, (tile, 2 * tile), 1) % tile
        col = lax.broadcasted_iota(jnp.int32, (tile, 2 * tile), 0)
        for j in range(i + 1):
            keys = slice(j * tile, (j + 1) * tile)
            block(q2, do2, logs, delta, k_ref[keys, :], v_ref[keys, :], col <= row if j == i else None, dk_s, dv_s, keys, j == 0)

        @pl.when(place > 0)
        def _():
            for j in range(before // tile):
                keys = slice(j * tile, (j + 1) * tile)
                seen = None
                if before > tokens:
                    seen = (lax.broadcasted_iota(jnp.int32, (tile, 2 * tile), 0) + j * tile) < place * tokens
                block(q2, do2, logs, delta, pk_ref[keys, :], pv_ref[keys, :], seen, dpk_s, dpv_s, keys, False)

        dq = dq_s[...]
        dq_ref[here, :] = jnp.where(low, dq[:tile], dq[tile:])

    dk_ref[...] = dk_s[...]
    dv_ref[...] = dv_s[...]
    dpk_ref[...] = dpk_s[...]
    dpv_ref[...] = dpv_s[...]


def attend_back(place, q, do, total, delta, kd, vd, pkd, pvd, tile):
    tokens, width = q.shape
    before = pkd.shape[0]
    pairs = width // 128
    at = lambda n, p: (0, n)
    row = lambda n, p: (n, 0, 0)
    return pl.pallas_call(
        functools.partial(attend_back_kernel, tile),
        grid_spec=pltpu.PrefetchScalarGridSpec(
            num_scalar_prefetch=1,
            grid=(pairs,),
            in_specs=[pl.BlockSpec((tokens, 128), at)] * 2
            + [pl.BlockSpec((1, 2, tokens), row)] * 2
            + [pl.BlockSpec((tokens, 128), at)] * 2
            + [pl.BlockSpec((before, 128), at)] * 2,
            out_specs=[pl.BlockSpec((tokens, 128), at)] * 3 + [pl.BlockSpec((before, 128), at)] * 2,
            scratch_shapes=[
                pltpu.VMEM((tokens, 128), F32),
                pltpu.VMEM((tokens, 128), F32),
                pltpu.VMEM((before, 128), F32),
                pltpu.VMEM((before, 128), F32),
                pltpu.VMEM((2 * tile, 128), F32),
            ],
        ),
        out_shape=[jax.ShapeDtypeStruct((tokens, width), F32)] * 3
        + [jax.ShapeDtypeStruct((before, width), F32)] * 2,
        compiler_params=pltpu.CompilerParams(vmem_limit_bytes=48 * 1024 * 1024),
        cost_estimate=pl.CostEstimate(
            flops=10 * width * tokens * (tokens + before) * 2, transcendentals=0, bytes_accessed=24 * tokens * width
        ),
        name="attend_back",
    )(place, q, do, total, delta, kd, vd, pkd, pvd)


def rank_mask(onehot, copies):
    widened = jnp.repeat(onehot, ADAPTER_RANK, axis=-1)
    return jnp.concatenate([widened] * copies, axis=-1)


def token_layout(row_position):
    past_prompt = jnp.maximum(row_position - PROMPT, 0)
    sequence = jnp.where(row_position < PROMPT, 0, 1 + past_prompt // CONT_LEN)
    position = jnp.where(row_position < PROMPT, row_position, PROMPT + past_prompt % CONT_LEN)
    return (sequence, position)


def rotary_table(position):
    half_width = HEAD_SIZE // 2
    frequency = jnp.exp(
        jnp.arange(half_width, dtype=jnp.float32) * (-2.0 * math.log(THETA) / HEAD_SIZE)
    )
    angle_table = position.astype(jnp.float32)[:, None] * frequency[None, :]
    return (jnp.cos(angle_table), jnp.sin(angle_table))


def rotate_halves(values, cosine_table, sine_table):
    half_width = HEAD_SIZE // 2
    first_half = values[..., :half_width]
    second_half = values[..., half_width:]
    cos_heads = cosine_table[:, None, :]
    sin_heads = sine_table[:, None, :]
    return jnp.concatenate(
        [
            first_half * cos_heads - second_half * sin_heads,
            second_half * cos_heads + first_half * sin_heads,
        ],
        axis=-1,
    )


def norm_back(grad_in, values, inverse, gain_row):
    scaled = grad_in * gain_row
    normed = values * inverse
    return inverse * (scaled - normed * jnp.mean(scaled * normed, axis=-1, keepdims=True))


def twice(x):
    rows = x.shape[0]
    return jnp.repeat(x.reshape(rows, KEY_HEADS, 1, HEAD_SIZE), 2, axis=2).reshape(rows, -1)


def fold(x):
    rows = x.shape[0]
    return x.reshape(rows, KEY_HEADS, 2, HEAD_SIZE).sum(axis=2).reshape(rows, -1)


def slot_rows(hit):
    tokens = hit.shape[1]
    before = (
        jnp.arange(tokens, dtype=jnp.int32)[:, None] < jnp.arange(tokens, dtype=jnp.int32)[None, :]
    ).astype(BF16)
    rank = dot_nn(hit.astype(BF16), before)
    return jnp.where(hit, rank.astype(jnp.int32), -1)


def swap(x):
    return lax.ppermute(x, "shard", [(0, 1), (1, 0)])


def local(
    layer_input,
    output_gradient,
    routes,
    sequence_adapter,
    attention_gain,
    experts_gain,
    project_weight,
    output_weight,
    router_weight,
    adapter_project_first,
    adapter_project_second,
    adapter_output_first,
    adapter_output_second,
    adapter_router_first,
    adapter_router_second,
    expert_gate_up_weight,
    expert_down_weight,
    adapter_expert_first,
    adapter_expert_second,
    adapter_expert_down_first,
    adapter_expert_down_second,
):
    shards = lax.axis_size("shard")
    me = lax.axis_index("shard")
    tokens = layer_input.shape[0]
    owned = expert_gate_up_weight.shape[0]
    rank = ADAPTER_POOL * ADAPTER_RANK
    qw = QUERY_HEADS * HEAD_SIZE
    kw = KEY_HEADS * HEAD_SIZE
    cap = tokens * TOPK // EXPERT_COUNT * 5 // 4
    cap = -(-cap // 16) * 16
    tile = min(256, tokens)
    scale = HEAD_SIZE ** (-0.5)
    pair = shards == 2

    project = lax.all_gather(project_weight, "shard", axis=1, tiled=True)
    firsts = lax.all_gather(
        jnp.concatenate(
            [adapter_project_first, adapter_output_first, adapter_router_first, router_weight], axis=1
        ),
        "shard", axis=0, tiled=True,
    )
    a_qkv, a_out, a_router, w_router = (
        firsts[:, : 3 * rank],
        firsts[:, 3 * rank : 4 * rank],
        firsts[:, 4 * rank : 5 * rank],
        firsts[:, 5 * rank :],
    )
    seconds = lax.all_gather(
        jnp.concatenate([adapter_project_second, adapter_output_second, adapter_router_second], axis=1),
        "shard", axis=0, tiled=False,
    )

    def columns(lo, width):
        return seconds[:, :, lo : lo + width].transpose(1, 0, 2).reshape(rank, shards * width)

    pw, ow, rw = adapter_project_second.shape[1], adapter_output_second.shape[1], adapter_router_second.shape[1]
    b_qkv, b_out, b_router = columns(0, pw), columns(pw, ow), columns(pw + ow, rw)
    w_out = lax.all_gather(output_weight, "shard", axis=0, tiled=True)

    local_rows = me * tokens + jnp.arange(tokens, dtype=jnp.int32)
    sequence, position = token_layout(local_rows)

    def adapters_of(seq):
        return jnp.sum(
            jnp.where(
                seq[:, None] == jnp.arange(sequence_adapter.shape[1], dtype=jnp.int32)[None, :],
                sequence_adapter,
                0,
            ),
            axis=1,
        )

    adapter = adapters_of(sequence)
    onehot = (adapter[:, None] == jnp.arange(ADAPTER_POOL, dtype=jnp.int32)[None, :]).astype(BF16)
    mask_one = rank_mask(onehot, 1)
    mask_three = rank_mask(onehot, 3)
    cosine_table, sine_table = rotary_table(position)

    if pair:
        blocks_routes = [routes, swap(routes)]
        other_rows = (1 - me) * tokens + jnp.arange(tokens, dtype=jnp.int32)
        labels = [adapter, adapters_of(token_layout(other_rows)[0])]
        grads_other = swap(output_gradient)
    else:
        everyone = lax.all_gather(routes, "shard", axis=0, tiled=False)
        blocks_routes = [everyone[j] for j in range(shards)]
        whole = adapters_of(token_layout(jnp.arange(shards * tokens, dtype=jnp.int32))[0])
        labels = [whole[j * tokens : (j + 1) * tokens] for j in range(shards)]
    mine = me * owned + jnp.arange(owned, dtype=jnp.int32)
    slots = [
        slot_rows(jnp.any(r.T[None, :, :] == mine[:, None, None], axis=1)).reshape(1, owned, 1, tokens)
        for r in blocks_routes
    ]
    labels = [l.astype(F32).reshape(1, 1, tokens) for l in labels]
    chosen = jnp.any(routes[:, :, None] == jnp.arange(EXPERT_COUNT, dtype=jnp.int32), axis=1)

    residual = layer_input.astype(F32)
    inverse_one = lax.rsqrt(jnp.mean(residual * residual, axis=-1, keepdims=True) + EPSILON)
    normed = (residual * inverse_one * attention_gain).astype(BF16)
    rank_qkv = (dot_nn(normed, a_qkv) * mask_three).astype(BF16)
    extra = jnp.concatenate(
        [
            dot_nn(rank_qkv[:, :rank], b_qkv[:, :qw]),
            dot_nn(rank_qkv[:, rank : 2 * rank], b_qkv[:, qw : qw + kw]),
            dot_nn(rank_qkv[:, 2 * rank :], b_qkv[:, qw + kw :]),
        ],
        axis=1,
    )
    pre = dot_nn(normed, project) + extra
    queries = (
        rotate_halves(pre[:, :qw].reshape(tokens, QUERY_HEADS, HEAD_SIZE), cosine_table, sine_table)
        .astype(BF16)
        .reshape(tokens, qw)
        * jnp.bfloat16(scale)
    )
    keys = (
        rotate_halves(pre[:, qw : qw + kw].reshape(tokens, KEY_HEADS, HEAD_SIZE), cosine_table, sine_table)
        .astype(BF16)
        .reshape(tokens, kw)
    )
    values = pre[:, qw + kw :].astype(BF16)
    keyval = jnp.concatenate([keys, values], axis=1)
    if pair:
        prior = lax.ppermute(keyval, "shard", [(0, 1)])
    else:
        prior = lax.all_gather(keyval, "shard", axis=0, tiled=True)
    key2, value2 = twice(keys), twice(values)
    prior_key2, prior_value2 = twice(prior[:, :kw]), twice(prior[:, kw:])
    place = me.astype(jnp.int32).reshape(1)
    mixed, log_total = attend(place, queries, key2, value2, prior_key2, prior_value2, tile)

    rank_out = (dot_nn(mixed, a_out) * mask_one).astype(BF16)
    hidden_one = residual + dot_nn(mixed, w_out) + dot_nn(rank_out, b_out)
    inverse_two = lax.rsqrt(jnp.mean(hidden_one * hidden_one, axis=-1, keepdims=True) + EPSILON)
    moe_in = (hidden_one * inverse_two * experts_gain).astype(BF16)
    rank_router = (dot_nn(moe_in, a_router) * mask_one).astype(BF16)
    logits = dot_nn(moe_in, w_router) + dot_nn(rank_router, b_router)
    peak = jnp.max(jnp.where(chosen, logits, -jnp.inf), axis=1, keepdims=True)
    weights = jnp.where(chosen, jnp.exp(jnp.where(chosen, logits, peak) - peak), 0.0)
    gates = weights / jnp.sum(weights, axis=1, keepdims=True)
    gates_t = gates.T
    grad_top = output_gradient.astype(F32)
    experts_weights = (
        expert_gate_up_weight,
        expert_down_weight,
        adapter_expert_first,
        adapter_expert_second,
        adapter_expert_down_first,
        adapter_expert_down_second,
    )
    if pair:
        half = owned // 2
        shape = (1, owned, 1, tokens)
        rows_other = swap(moe_in)
        gates_own = lax.dynamic_slice_in_dim(gates_t, me * owned, owned, 0).reshape(shape)
        gates_other = swap(lax.dynamic_slice_in_dim(gates_t, (1 - me) * owned, owned, 0)).reshape(shape)
        own = (moe_in, output_gradient, slots[0], gates_own, labels[0], experts_weights, cap)
        other = (rows_other, grads_other, slots[1], gates_other, labels[1], experts_weights, cap)
        out_a, back_a, dg_a, lora_a = experts(*own, 0, half)
        out_b, back_b, dg_b, lora_low = experts(*other, 0, half, lora=lora_a, lora_type=BF16)
        out_c, back_c, dg_c, lora_c = experts(*other, half, half, acc=(out_b, back_b), acc_type=BF16)
        out_own, back_own, dg_d, lora_high = experts(
            *own, half, half, acc=(out_a, back_a), lora=lora_c, lora_type=BF16
        )
        back_got, dg_got = swap(back_c), swap(jnp.concatenate([dg_b, dg_c], axis=1))
        out_got = swap(out_c)
        combined = out_own + out_got.astype(F32)
        grad_moe = back_own + back_got.astype(F32)
        dg_own = jnp.concatenate([dg_a, dg_d], axis=1).reshape(owned, tokens)
        dg_got = dg_got.reshape(owned, tokens)
        dg_t = jnp.concatenate(
            [jnp.where(me == 0, dg_own, dg_got), jnp.where(me == 0, dg_got, dg_own)], axis=0
        )
        low_total = lax.psum(lora_low, "rep")
        lora_high, low_total = lax.optimization_barrier((lora_high, low_total))
        lora_total = jnp.concatenate([low_total, lax.psum(lora_high, "rep")], axis=0)
    else:
        rows_all = lax.all_gather(moe_in, "shard", axis=0, tiled=True)
        grads_all = lax.all_gather(output_gradient, "shard", axis=0, tiled=True)
        gates_all = lax.dynamic_slice_in_dim(
            lax.all_gather(gates_t, "shard", axis=0, tiled=False), me * owned, owned, 1
        ).reshape(shards, owned, 1, tokens)
        out_p, back_p, dg_p, lora_p = experts(
            rows_all, grads_all, jnp.concatenate(slots, axis=0), gates_all, jnp.concatenate(labels, axis=0),
            experts_weights, cap, 0, owned, acc_type=BF16,
        )
        combined = lax.psum_scatter(out_p, "shard", scatter_dimension=0, tiled=True).astype(F32)
        grad_moe = lax.psum_scatter(back_p, "shard", scatter_dimension=0, tiled=True).astype(F32)
        dg_all = lax.all_gather(dg_p.reshape(shards, owned, tokens), "shard", axis=0, tiled=False)
        dg_t = lax.dynamic_index_in_dim(dg_all, me, 1, keepdims=False).reshape(EXPERT_COUNT, tokens)
        lora_total = lax.psum(
            lora_p.reshape((shards, owned) + lora_p.shape[1:]).sum(axis=0).astype(BF16), "rep"
        )
    block_out = (hidden_one + combined).astype(BF16)

    dgates = dg_t.T
    dpicked = gates * (dgates - jnp.sum(dgates * gates, axis=-1, keepdims=True))
    grad_logits = dpicked.astype(BF16)
    grad_out_router = dot_tn(rank_router, grad_logits)
    grad_rank_router = dot_nt(grad_logits, b_router).astype(BF16) * mask_one
    grad_in_router = dot_tn(moe_in, grad_rank_router)
    grad_moe = grad_moe + dot_nt(grad_logits, w_router) + dot_nt(grad_rank_router, a_router)
    grad_hidden = grad_top + norm_back(grad_moe, hidden_one, inverse_two, experts_gain)
    grad_branch = grad_hidden.astype(BF16)
    grad_out_out = dot_tn(rank_out, grad_branch)
    grad_rank_out = dot_nt(grad_branch, b_out).astype(BF16) * mask_one
    grad_in_out = dot_tn(mixed, grad_rank_out)
    grad_mixed = (dot_nt(grad_branch, w_out) + dot_nt(grad_rank_out, a_out)).astype(BF16)
    delta = (
        (mixed.astype(F32) * grad_mixed.astype(F32))
        .reshape(tokens, KEY_HEADS, 2, HEAD_SIZE)
        .sum(axis=-1)
        .transpose(1, 2, 0)
    )
    dq, dk2, dv2, dpk2, dpv2 = attend_back(
        place, queries, grad_mixed, log_total, delta, key2, value2, prior_key2, prior_value2, tile
    )
    sent = jnp.concatenate([fold(dpk2), fold(dpv2)], axis=1).astype(BF16)
    if pair:
        got = lax.ppermute(sent, "shard", [(1, 0)]).astype(F32)
    else:
        got = lax.psum_scatter(sent, "shard", scatter_dimension=0, tiled=True).astype(F32)
    dk = fold(dk2) + got[:, :kw]
    dv = fold(dv2) + got[:, kw:]
    dq_pre = rotate_halves(
        (dq * scale).reshape(tokens, QUERY_HEADS, HEAD_SIZE), cosine_table, -sine_table
    ).reshape(tokens, qw)
    dk_pre = rotate_halves(
        dk.reshape(tokens, KEY_HEADS, HEAD_SIZE), cosine_table, -sine_table
    ).reshape(tokens, kw)
    grad_pre = jnp.concatenate([dq_pre, dk_pre, dv], axis=1).astype(BF16)
    gq, gk, gv = grad_pre[:, :qw], grad_pre[:, qw : qw + kw], grad_pre[:, qw + kw :]
    grad_out_qkv = jnp.concatenate(
        [
            dot_tn(rank_qkv[:, :rank], gq),
            dot_tn(rank_qkv[:, rank : 2 * rank], gk),
            dot_tn(rank_qkv[:, 2 * rank :], gv),
        ],
        axis=1,
    )
    grad_rank_qkv = (
        jnp.concatenate(
            [
                dot_nt(gq, b_qkv[:, :qw]),
                dot_nt(gk, b_qkv[:, qw : qw + kw]),
                dot_nt(gv, b_qkv[:, qw + kw :]),
            ],
            axis=1,
        ).astype(BF16)
        * mask_three
    )
    grad_in_qkv = dot_tn(normed, grad_rank_qkv)
    grad_normed = dot_nt(grad_pre, project) + dot_nt(grad_rank_qkv, a_qkv)
    input_grad = (grad_hidden + norm_back(grad_normed, residual, inverse_one, attention_gain)).astype(BF16)

    rows = layer_input.shape[1] // shards

    def reduced(parts):
        flat = jnp.concatenate([p.astype(BF16).reshape(-1) for p in parts]).reshape(-1, 128)
        total = lax.psum(flat, ("rep", "shard")).reshape(-1)
        outs, at = [], 0
        for p in parts:
            outs.append(total[at : at + p.size].reshape(p.shape).astype(F32))
            at += p.size
        return outs

    t_in_out, t_out_out, t_in_router, t_out_router = reduced(
        [grad_in_out, grad_out_out, grad_in_router, grad_out_router]
    )
    grad_in_qkv, t_out_out = lax.optimization_barrier((grad_in_qkv, t_out_out))
    t_in_qkv, t_out_qkv = reduced([grad_in_qkv, grad_out_qkv])

    def part(x, axis):
        size = x.shape[axis] // shards
        return lax.dynamic_slice_in_dim(x, me * size, size, axis)

    total = lora_total.astype(F32)
    hidden = EXPERT_HIDDEN
    down_t = jnp.concatenate([total[:, 4 * rank :, :hidden], total[:, 4 * rank :, hidden:]], axis=1)
    return (
        block_out,
        input_grad,
        part(t_in_qkv, 0),
        part(t_out_qkv, 1),
        part(t_in_out, 0),
        part(t_out_out, 1),
        part(t_in_router, 0),
        part(t_out_router, 1),
        total[:, : 2 * rank].swapaxes(1, 2),
        total[:, 2 * rank : 3 * rank],
        down_t.swapaxes(1, 2),
        total[:, 3 * rank : 4 * rank],
    )


def solution(mesh):
    return jax.shard_map(
        local,
        mesh=mesh,
        in_specs=(
            P(("rep", "shard"), None),
            P(("rep", "shard"), None),
            P(("rep", "shard"), None),
            P("rep", None),
            P(),
            P(),
            P(None, "shard"),
            P("shard", None),
            P("shard", None),
            P("shard", None),
            P(None, "shard"),
            P("shard", None),
            P(None, "shard"),
            P("shard", None),
            P(None, "shard"),
            P("shard", None, None),
            P("shard", None, None),
            P("shard", None, None),
            P("shard", None, None),
            P("shard", None, None),
            P("shard", None, None),
        ),
        out_specs=(
            P(("rep", "shard"), None),
            P(("rep", "shard"), None),
            P("shard", None),
            P(None, "shard"),
            P("shard", None),
            P(None, "shard"),
            P("shard", None),
            P(None, "shard"),
            P("shard", None, None),
            P("shard", None, None),
            P("shard", None, None),
            P("shard", None, None),
        ),
        check_vma=False,
    )
```

time: 2070 us -> 1020 us (0.49)
  matrix products: 581 us -> 53 us
  local copies, waits for them, and re-layouts: 399 us -> 107 us
  Pallas kernels: 0 us -> 260 us
  other arithmetic: 234 us -> 50.3 us
  waiting for transfers between devices: 573 us -> 406 us
  blocking collectives: 199 us -> 87.5 us
    dot_general x105 -> x32, matrix products: 581 us -> 53 us  [the longest x11 23.5 us: dot_nt(): lax.dot_general(a, b, (((1,), (1,)), ((), ())), preferred_element_type=F32)]
    all_to_all x5 -> x0, waiting for transfers between devices: 314 us -> none  [the longest x1 122 us: local(): lax.all_to_all(grad_send, 'shard', split_axis=0, concat_axis=2, tiled=True)]
    pallas_call x0 -> x6, Pallas kernels: none -> 260 us  [the longest x4 209 us: experts(): pl.pallas_call(functools.partial(expert_kernel, acc is not None, lora is...]
    psum x1 -> x4, waiting for transfers between devices: 157 us -> 386 us  [the longest x2 173 us: reduced(): total = lax.psum(flat, ('rep', 'shard')).reshape(-1)]
    gather x6 -> x0, local copies, waits for them, and re-layouts: 203 us -> none  [the longest x1 39.8 us: local(): gate_ext[slot_assign][:, None]]
    convert_element_type x23 -> x12, other arithmetic: 119 us -> 13.3 us  [the longest x1 4.76 us: local(): total = lora_total.astype(F32)]
    all_gather x7 -> x2, blocking collectives: 165 us -> 87.5 us  [the longest x1 75.9 us: local(): lax.all_gather(jnp.concatenate([adapter_project_first, adapter_output_fir...]
    reduce_scatter x8 -> x0, waiting for transfers between devices: 64.6 us -> none  [the longest x1 16.1 us: local(): lax.psum_scatter(grad_in_qkv_full.astype(jnp.bfloat16), 'shard', scatter_...]
  transfers between devices with their start and end apart: 18 -> 15, of which waited for: 11 -> 5; matrix products, arithmetic and copies ran while one was open for 29% -> 16% of each run, Pallas kernels for 0% -> 15%
where the time goes in v1:
time: 1020 us
  waiting for transfers between devices  406 us (40%)
  Pallas kernels  260 us (25%)
  local copies, waits for them, and re-layouts  107 us (10%)
  blocking collectives  87.5 us (9%)
  matrix products  53 us (5%)
  other arithmetic  50.3 us (5%)
  starting transfers between devices  38.1 us (4%)
  between operations  15.6 us (2%)
    pallas_call x4, Pallas kernels, experts(): pl.pallas_call(functools.partial(expert_kernel, acc is not None, lora is...  209 us
    psum x2, waiting for transfers between devices, reduced(): total = lax.psum(flat, ('rep', 'shard')).reshape(-1)  173 us
    psum x1, waiting for transfers between devices, local(): lax.psum(lora_high, 'rep')  115 us
    psum x1, waiting for transfers between devices, local(): low_total = lax.psum(lora_low, 'rep')  98.1 us
    all_gather x1, blocking collectives, local(): lax.all_gather(jnp.concatenate([adapter_project_first, adapter_output_fir...  75.9 us
    ppermute x7, starting transfers between devices, swap(): return lax.ppermute(x, 'shard', [(0, 1), (1, 0)])  31.9 us
    unnamed x146, local copies, waits for them, and re-layouts  28.7 us
    pallas_call x1, Pallas kernels, attend_back(): pl.pallas_call(functools.partial(attend_back_kernel, tile), grid_spec=plt...  28.4 us
  transfers between devices with their start and end apart: 15, of which 5 were waited for; matrix products, arithmetic and copies ran while one was open for 16% of the time, Pallas kernels for 15%

profile of v1, /device:TPU:0, one launch (start us, length us, event | category | flops | bytes accessed | tf_op | source)
XLA Modules:
  0.0 1017.2 jit_solution(5612753974332265298)
XLA Ops:
  8.1 3.0 collective-permute-start.3
  11.3 75.9 %all_gather.16 = bf16[1024,352]{0,1:T(8,128)(2,1)S(1)} all-gather(bf16[512,352]{0,1:T(8,128)(2,1)S(1)} %pad_maximum_fusion.4), channel_id=1, replica_groups=mesh['rep'=16,'shard'=2] {'shard'}, dimensions={0}, use_global_device_ids=true | all-gather | bytes 1081344 | tf_op jit(solution)/shard_map/all_gather | solution.py:490
  87.9 11.7 %all-gather = bf16[128,1552]{1,0:T(8,128)(2,1)S(1)} all-gather(bf16[64,1552]{1,0:T(8,128)(2,1)S(1)} %pad_maximum_fusion.6), channel_id=2, replica_groups=mesh['rep'=16,'shard'=2] {'shard'}, dimensions={0}, use_global_device_ids=true | all-gather | bytes 595968 | tf_op jit(solution)/shard_map/all_gather | solution.py:502
  104.2 2.3 fusion.44
  107.6 7.1 maximum_add_fusion
  121.8 4.4 collective-permute-start
  128.8 2.7 copy.173.down_first_ref
  134.2 4.0 slice.183
  139.3 2.4 copy.153
  147.8 2.6 copy.160.k_ref
  153.3 18.0 %collective-permute-done = bf16[768,1024]{1,0:T(8,128)(2,1)} collective-permute-done((bf16[768,1024]{1,0:T(8,128)(2,1)}, bf16[768,1024]{1,0:T(8,128)(2,1)}, u32[]{:S(2)}, u32[]{:S(2)}) %collective-permute-start) | collective-permute-done | bytes 1572896 | tf_op jit(solution)/shard_map/ppermute | solution.py:578
  171.3 2.4 fusion.90
  177.7 2.3 copy.158
  184.4 22.1 %attend.1 = (bf16[768,1024]{1,0:T(8,128)(2,1)S(1)}, f32[8,2,768]{2,1,0:T(2,128)S(1)}) custom-call(s32[1]{0:T(128)} %bitcast.place_ref, bf16[768,1024]{1,0:T(8,128)(2,1)S(1)} %copy.159.q_ref, bf16[768,1024]{1,0:T(8,128)(2,1)S(1)} %copy-done.2, bf16[768,1024]{1,0:T(8,128)(2,1)} %copy.161.v_ref, bf16[768,1024]{1,0:T(8,128)(2,1)} %copy.162.pk_ref, ...), custom_call_target="tpu_custom_call" | custom-call | flops 9663676416 | bytes 6291456 | tf_op jit(solution)/shard_map/attend/pallas_call | solution.py:272
  208.0 3.5 fusion.91
  216.3 24.7 %collective-permute-start.1 = (bf16[768,1024]{1,0:T(8,128)(2,1)S(1)}, bf16[768,1024]{1,0:T(8,128)(2,1)S(1)}, u32[]{:S(2)}, u32[]{:S(2)}) collective-permute-start(bf16[768,1024]{1,0:T(8,128)(2,1)S(1)} %multiply_convert_fusion.rows_ref), channel_id=1, source_target_pairs={{0,1},{1,0},{2,3},{3,2},{4,5},{5,4},{6,7},{7,6},{8,9},{9,8},{10,11... | collective-permute-start | bytes 4718600 | tf_op jit(solution)/shard_map/ppermute | solution.py:450
  242.0 51.7 %experts.4 = (f32[768,1024]{1,0:T(8,128)}, f32[768,1024]{1,0:T(8,128)}, f32[1,8,1,768]{3,2,1,0:T(1,128)}, f32[8,288,1024]{2,1,0:T(8,128)}) custom-call(bf16[768,1024]{1,0:T(8,128)(2,1)} %copy-done.9, bf16[768,1024]{1,0:T(8,128)(2,1)} %grad_ref.3, s32[1,16,1,768]{3,2,1,0:T(1,128)} %reshape.370.slot_ref, f32[1,16,1,768]{3,2,1,0:T(1,128)} %reshape.372.gate_ref, ...), custom_call_target="tpu_custom_call" | custom-call | flops 28689039360 | bytes 32000000 | tf_op jit(solution)/shard_map/experts/pallas_call | solution.py:180
  296.3 51.5 %experts.5 = (f32[768,1024]{1,0:T(8,128)}, f32[768,1024]{1,0:T(8,128)}, f32[1,8,1,768]{3,2,1,0:T(1,128)}, bf16[8,288,1024]{2,1,0:T(8,128)(2,1)}) custom-call(bf16[768,1024]{1,0:T(8,128)(2,1)} %copy-done.64, bf16[768,1024]{1,0:T(8,128)(2,1)} %collective-permute-done.2.grad_ref, s32[1,16,1,768]{3,2,1,0:T(1,128)} %copy.170.slot_ref, ...), custom_call_target="tpu_custom_call" | custom-call | flops 28689039360 | bytes 32000000 | tf_op jit(solution)/shard_map/experts/pallas_call | solution.py:180
  347.8 52.2 %experts.6 = (bf16[768,1024]{1,0:T(8,128)(2,1)}, bf16[768,1024]{1,0:T(8,128)(2,1)}, f32[1,8,1,768]{3,2,1,0:T(1,128)}, f32[8,288,1024]{2,1,0:T(8,128)}) custom-call(bf16[768,1024]{1,0:T(8,128)(2,1)} %copy-done.64, bf16[768,1024]{1,0:T(8,128)(2,1)} %collective-permute-done.2.grad_ref, s32[1,16,1,768]{3,2,1,0:T(1,128)} %copy.170.slot_ref, ...), custom_call_target="tpu_custom_call" | custom-call | flops 28689039360 | bytes 32000000 | tf_op jit(solution)/shard_map/experts/pallas_call | solution.py:180
  400.8 2.1 collective-permute-start.7
  404.9 53.7 %experts.7 = (f32[768,1024]{1,0:T(8,128)}, f32[768,1024]{1,0:T(8,128)}, f32[1,8,1,768]{3,2,1,0:T(1,128)}, bf16[8,288,1024]{2,1,0:T(8,128)(2,1)}) custom-call(bf16[768,1024]{1,0:T(8,128)(2,1)} %copy-done.9, bf16[768,1024]{1,0:T(8,128)(2,1)} %grad_ref.3, s32[1,16,1,768]{3,2,1,0:T(1,128)} %reshape.370.slot_ref, f32[1,16,1,768]{3,2,1,0:T(1,128)} %reshape.372.gate_ref, ...), custom_call_target="tpu_custom_call" | custom-call | flops 28689039360 | bytes 32000000 | tf_op jit(solution)/shard_map/experts/pallas_call | solution.py:180
  468.9 3.7 multiply_reduce_fusion
  472.7 3.3 multiply_add_fusion
  481.8 5.2 convert_multiply_fusion.2
  487.0 3.8 copy.178
  490.8 2.3 bitcast_reduce_fusion
  493.7 28.4 %attend_back.1 = (f32[768,1024]{1,0:T(8,128)}, f32[768,1024]{1,0:T(8,128)}, f32[768,1024]{1,0:T(8,128)}, f32[768,1024]{1,0:T(8,128)}, f32[768,1024]{1,0:T(8,128)}) custom-call(s32[1]{0:T(128)} %bitcast.place_ref, bf16[768,1024]{1,0:T(8,128)(2,1)S(1)} %copy-done.1, bf16[768,1024]{1,0:T(8,128)(2,1)S(1)} %get-tuple-element.151.do_ref, ...), custom_call_target="tpu_custom_call" | custom-call | flops 24159191040 | bytes 18874368 | tf_op jit(solution)/shard_map/attend_back/pallas_call | solution.py:360
  522.1 2.4 copy.187
  524.5 3.6 copy.186
  529.4 2.2 reduce_sum.126
  534.6 4.0 copy.185
  538.6 3.4 reduce_sum.125
  542.1 3.5 copy.188
  545.6 3.4 reduce_sum.128
  549.0 2.4 copy.184
  551.4 2.4 subtract_convert_fusion
  555.0 2.1 convolution_convert_fusion.2
  557.1 48.7 %all-reduce.5.cloned.1.call-done = bf16[1552,128]{1,0:T(8,128)(2,1)} async-done(((bf16[1552,128]{1,0:T(8,128)(2,1)}), bf16[1552,128]{1,0:T(8,128)(2,1)}) %all-reduce.5.cloned.1.call-update) | async-done | bytes 397328 | tf_op jit(solution)/shard_map/psum | solution.py:714
  624.0 2.4 reshape.393
  630.1 98.1 %all-reduce.9.cloned.1.call-done = bf16[8,288,1024]{2,1,0:T(8,128)(2,1)} async-done(((bf16[8,288,1024]{2,1,0:T(8,128)(2,1)}), bf16[8,288,1024]{2,1,0:T(8,128)(2,1)}) %all-reduce.9.cloned.1.call-update) | async-done | bytes 4718608 | tf_op jit(solution)/shard_map/psum | solution.py:628
  730.8 6.2 fusion.4
  739.0 124.1 %all-reduce.7.cloned.1.call-done = bf16[2560,128]{1,0:T(8,128)(2,1)} async-done(((bf16[2560,128]{1,0:T(8,128)(2,1)}), bf16[2560,128]{1,0:T(8,128)(2,1)}) %all-reduce.7.cloned.1.call-update) | async-done | bytes 655376 | tf_op jit(solution)/shard_map/psum | solution.py:714
  867.2 115.5 %all-reduce.11.cloned.1.call-done = bf16[8,288,1024]{2,1,0:T(8,128)(2,1)} async-done(((bf16[8,288,1024]{2,1,0:T(8,128)(2,1)}), bf16[8,288,1024]{2,1,0:T(8,128)(2,1)}) %all-reduce.11.cloned.1.call-update) | async-done | bytes 4718608 | tf_op jit(solution)/shard_map/psum | solution.py:630
  982.7 4.8 maximum_convert_fusion
  987.4 4.2 slice_bitcast_fusion
  991.6 2.3 slice.210
  993.9 9.2 copy.197
  1006.1 4.0 maximum_convert_fusion.1
  (292 shorter events, 105.8 us)
Async XLA Ops:
  7.2 4.1 copy-start.55
  7.2 4.1 copy-start.51
  7.2 4.1 copy-start.52
  7.2 4.1 copy-start.47
  7.2 80.0 %copy-start.63 = (s32[1,2]{1,0:T(1,128)S(1)}, s32[1,2]{1,0:T(1,128)}, u32[]{:S(2)}) copy-start(s32[1,2]{1,0:T(1,128)} %param.24) | copy-start | bytes 28
  7.2 80.1 %copy-start.11 = (bf16[768,1024]{1,0:T(8,128)(2,1)S(1)}, bf16[768,1024]{1,0:T(8,128)(2,1)}, u32[]{:S(2)}) copy-start(bf16[768,1024]{1,0:T(8,128)(2,1)} %param.21) | copy-start | bytes 4718596
  7.2 80.5 %copy-start.62 = (bf16[64,16]{0,1:T(8,128)(2,1)S(1)}, bf16[64,16]{0,1:T(8,128)(2,1)}, u32[]{:S(2)}) copy-start(bf16[64,16]{0,1:T(8,128)(2,1)} %param.35) | copy-start | bytes 6148
  7.3 80.6 %copy-start.50 = (bf16[64,512]{1,0:T(8,128)(2,1)S(1)}, bf16[64,512]{1,0:T(8,128)(2,1)}, u32[]{:S(2)}) copy-start(bf16[64,512]{1,0:T(8,128)(2,1)} %param.33) | copy-start | bytes 196612
  7.3 80.6 %copy-start.48 = (bf16[64,1024]{1,0:T(8,128)(2,1)S(1)}, bf16[64,1024]{1,0:T(8,128)(2,1)}, u32[]{:S(2)}) copy-start(bf16[64,1024]{1,0:T(8,128)(2,1)} %param.31) | copy-start | bytes 393220
  7.3 100.3 %all-gather.4.cloned.1.call-start = ((), (), s32[]{:S(2)}) async-start(), calls=%async_computation | async-start | bytes 6291456 | tf_op jit(solution)/shard_map/all_gather | solution.py:489
  8.0 92.4 %copy-start.65 = (f32[1024]{0:T(1024)S(1)}, f32[1024]{0:T(1024)}, u32[]{:S(2)}) copy-start(f32[1024]{0:T(1024)} %param.25) | copy-start | bytes 12292
  8.0 199.9 %all-gather.6.cloned.1.call-start = ((), (), s32[]{:S(2)}) async-start(), calls=%async_computation.1 | async-start | bytes 3145728 | tf_op jit(solution)/shard_map/all_gather | solution.py:512
  8.1 124.0 %collective-permute-start.3 = (s32[768,8]{0,1:T(8,128)}, s32[768,8]{0,1:T(8,128)S(1)}, u32[]{:S(2)}, u32[]{:S(2)}) collective-permute-start(s32[768,8]{0,1:T(8,128)} %param.23), channel_id=1, source_target_pairs={{0,1},{1,0},{2,3},{3,2},{4,5},{5,4},{6,7},{7,6},{8,9},{9,8},{10,11... | collective-permute-start | bytes 73736 | tf_op jit(solution)/shard_map/ppermute | solution.py:450
  11.1 284.0 %collective-permute-start.2 = (bf16[768,1024]{1,0:T(8,128)(2,1)}, bf16[768,1024]{1,0:T(8,128)(2,1)}, u32[]{:S(2)}, u32[]{:S(2)}) collective-permute-start(bf16[768,1024]{1,0:T(8,128)(2,1)} %grad_ref.3), channel_id=1, source_target_pairs={{0,1},{1,0},{2,3},{3,2},{4,5},{5,4},{6,7},{7,6},{8,9},{9,8},{10,11... | collective-permute-start | bytes 4718600 | tf_op jit(solution)/shard_map/ppermute | solution.py:450
  11.2 594.6 %all-reduce.5.cloned.1.call-start = ((), (), s32[]{:S(2)}) async-start(), calls=%async_computation.2 | async-start | bytes 794624 | tf_op jit(solution)/shard_map/psum | solution.py:714
  87.2 14.0 %copy-start.23 = (bf16[1024,352]{0,1:T(8,128)(2,1)}, bf16[1024,352]{0,1:T(8,128)(2,1)S(1)}, u32[]{:S(2)}) copy-start(bf16[1024,352]{0,1:T(8,128)(2,1)S(1)} %all_gather.16) | copy-start | bytes 2162692
  87.7 19.8 %copy-start.60 = (f32[768]{0:T(1024)}, f32[768]{0:T(1024)S(1)}, u32[]{:S(2)}) copy-start(f32[768]{0:T(1024)S(1)} %add_rsqrt_fusion.1) | copy-start | bytes 9220
  100.3 3.9 copy-start.29
  101.2 5.3 copy-start.34
  107.6 12.3 %copy-start.38 = (f32[768,32]{0,1:T(8,128)}, f32[768,32]{0,1:T(8,128)S(1)}, u32[]{:S(2)}) copy-start(f32[768,32]{0,1:T(8,128)S(1)} %get-tuple-element.142) | copy-start | bytes 294916
  107.6 34.1 %copy-start.27 = (f32[768,32]{0,1:T(8,128)}, f32[768,32]{0,1:T(8,128)S(1)}, u32[]{:S(2)}) copy-start(f32[768,32]{0,1:T(8,128)S(1)} %get-tuple-element.143) | copy-start | bytes 294916
  120.1 6.2 copy-start.49
  120.2 11.3 %copy-start.14 = (bf16[768,8,64]{0,2,1:T(8,128)(2,1)}, bf16[768,8,64]{0,2,1:T(8,128)(2,1)S(1)}, u32[]{:S(2)}) copy-start(bf16[768,8,64]{0,2,1:T(8,128)(2,1)S(1)} %maximum_convert_fusion.2) | copy-start | bytes 2359300
  121.8 49.4 %collective-permute-start = (bf16[768,1024]{1,0:T(8,128)(2,1)}, bf16[768,1024]{1,0:T(8,128)(2,1)}, u32[]{:S(2)}, u32[]{:S(2)}) collective-permute-start(bf16[768,1024]{1,0:T(8,128)(2,1)} %pad_maximum_fusion), channel_id=1, source_target_pairs={{0,1},{2,3},{4,5},{6,7},{8,9},{10,11},{12,13},{14,15},{16,17},{18,... | collective-permute-start | bytes 4718600 | tf_op jit(solution)/shard_map/ppermute | solution.py:578
  146.3 36.6 %copy-start = (bf16[768,1024]{1,0:T(8,128)(2,1)}, bf16[768,1024]{1,0:T(8,128)(2,1)S(1)}, u32[]{:S(2)}) copy-start(bf16[768,1024]{1,0:T(8,128)(2,1)S(1)} %copy.159.q_ref) | copy-start | bytes 4718596
  207.9 3.5 copy-start.12
  213.3 28.6 %copy-start.9 = (bf16[768,1024]{1,0:T(8,128)(2,1)}, bf16[768,1024]{1,0:T(8,128)(2,1)S(1)}, u32[]{:S(2)}) copy-start(bf16[768,1024]{1,0:T(8,128)(2,1)S(1)} %multiply_convert_fusion.rows_ref) | copy-start | bytes 4718596
  216.3 78.7 %collective-permute-start.1 = (bf16[768,1024]{1,0:T(8,128)(2,1)S(1)}, bf16[768,1024]{1,0:T(8,128)(2,1)S(1)}, u32[]{:S(2)}, u32[]{:S(2)}) collective-permute-start(bf16[768,1024]{1,0:T(8,128)(2,1)S(1)} %multiply_convert_fusion.rows_ref), channel_id=1, source_target_pairs={{0,1},{1,0},{2,3},{3,2},{4,5},{5,4},{6,7},{7,6},{8,9},{9,8},{10,11... | collective-permute-start | bytes 4718600 | tf_op jit(solution)/shard_map/ppermute | solution.py:450
  241.9 52.5 %collective-permute-start.4 = (f32[16,768]{1,0:T(8,128)S(1)}, f32[16,768]{1,0:T(8,128)S(1)}, u32[]{:S(2)}, u32[]{:S(2)}) collective-permute-start(f32[16,768]{1,0:T(8,128)S(1)} %get-tuple-element.139), channel_id=1, source_target_pairs={{0,1},{1,0},{2,3},{3,2},{4,5},{5,4},{6,7},{7,6},{8,9},{9,8},{10,11... | collective-permute-start | bytes 147464 | tf_op jit(solution)/shard_map/ppermute | solution.py:450
  347.8 53.0 %copy-start.56 = (f32[1,8,1,768]{3,2,1,0:T(1,128)S(1)}, f32[1,8,1,768]{3,2,1,0:T(1,128)}, u32[]{:S(2)}) copy-start(f32[1,8,1,768]{3,2,1,0:T(1,128)} %get-tuple-element.52) | copy-start | bytes 73732
  400.8 58.6 %collective-permute-start.7 = (f32[1,16,1,768]{3,1,2,0:T(8,128)S(1)}, f32[1,16,1,768]{3,1,2,0:T(8,128)S(1)}, u32[]{:S(2)}, u32[]{:S(2)}) collective-permute-start(f32[1,16,1,768]{3,1,2,0:T(8,128)S(1)} %pad_maximum_fusion.7), channel_id=1, source_target_pairs={{0,1},{1,0},{2,3},{3,2},{4,5},{5,4},{6,7},{7,6},{8,9},{9,8},{10,11... | collective-permute-start | bytes 147464 | tf_op jit(solution)/shard_map/ppermute | solution.py:450
  402.9 65.7 %collective-permute-start.6 = (bf16[768,1024]{1,0:T(8,128)(2,1)}, bf16[768,1024]{1,0:T(8,128)(2,1)}, u32[]{:S(2)}, u32[]{:S(2)}) collective-permute-start(bf16[768,1024]{1,0:T(8,128)(2,1)} %get-tuple-element.49), channel_id=1, source_target_pairs={{0,1},{1,0},{2,3},{3,2},{4,5},{5,4},{6,7},{7,6},{8,9},{9,8},{10,11... | collective-permute-start | bytes 4718600 | tf_op jit(solution)/shard_map/ppermute | solution.py:450
  403.0 69.7 %collective-permute-start.5 = (bf16[768,1024]{1,0:T(8,128)(2,1)}, bf16[768,1024]{1,0:T(8,128)(2,1)}, u32[]{:S(2)}, u32[]{:S(2)}) collective-permute-start(bf16[768,1024]{1,0:T(8,128)(2,1)} %get-tuple-element.47), channel_id=1, source_target_pairs={{0,1},{1,0},{2,3},{3,2},{4,5},{5,4},{6,7},{7,6},{8,9},{9,8},{10,11... | collective-permute-start | bytes 4718600 | tf_op jit(solution)/shard_map/ppermute | solution.py:450
  404.9 59.1 %copy-start.10 = (bf16[768,1024]{1,0:T(8,128)(2,1)S(1)}, bf16[768,1024]{1,0:T(8,128)(2,1)}, u32[]{:S(2)}) copy-start(bf16[768,1024]{1,0:T(8,128)(2,1)} %copy-done.9) | copy-start | bytes 4718596
  460.8 7.8 copy-start.54
  460.8 7.8 copy-start.58
  468.9 3.8 copy-start.26
  468.9 3.8 copy-start.33
  479.2 249.0 %all-reduce.9.cloned.1.call-start = ((), (), s32[]{:S(2)}) async-start(), calls=%async_computation.4 | async-start | bytes 9437184 | tf_op jit(solution)/shard_map/psum | solution.py:628
  479.8 383.3 %all-reduce.7.cloned.1.call-start = ((), (), s32[]{:S(2)}) async-start(), calls=%async_computation.3 | async-start | bytes 1310720 | tf_op jit(solution)/shard_map/psum | solution.py:714
  532.9 81.8 %collective-permute-start.8 = (bf16[768,1024]{0,1:T(8,128)(2,1)}, bf16[768,1024]{0,1:T(8,128)(2,1)}, u32[]{:S(2)}, u32[]{:S(2)}) collective-permute-start(bf16[768,1024]{0,1:T(8,128)(2,1)} %pad_maximum_fusion.2), channel_id=1, source_target_pairs={{1,0},{3,2},{5,4},{7,6},{9,8},{11,10},{13,12},{15,14},{17,16},{19,... | collective-permute-start | bytes 4718600 | tf_op jit(solution)/shard_map/ppermute | solution.py:674
  609.3 7.2 copy-start.20
  617.3 3.3 copy-start.13
  617.3 3.3 copy-start.44
  617.3 3.3 copy-start.61
  617.3 3.3 copy-start.66
  628.4 354.3 %all-reduce.11.cloned.1.call-start = ((), (), s32[]{:S(2)}) async-start(), calls=%async_computation.5 | async-start | bytes 9437184 | tf_op jit(solution)/shard_map/psum | solution.py:630
  730.8 6.3 copy-start.6
  (34 other events, 63.5 us)
Sparse Core Ops, SparseCore 0:
  9.7 94.9 all-gather.3
  106.2 45.4 all-gather.5
  479.4 126.3 all-reduce.4
  610.3 117.9 all-reduce.8
  734.7 128.3 all-reduce.6
  866.6 116.0 all-reduce.10
